TPU v7x, 512 devices: a whole 4x4x16 slice. The times are simulated.
512 devices in a mesh: vis: 4 (over y_lo, core), row: 16 (over z), col: 8 (over y_hi, x).
Axes of the slice: x: 4, y: 4 (y_hi: 2, y_lo: 2; y = y_hi * 2 + y_lo), z: 16, core: 2. Of those that a mesh axis runs over, the one named last changes fastest.
Arguments:
- partials: bfloat16 [4, 2, 8192, 8192], P('vis', None, 'row', 'col'), may hold values from -6 to 6
- coverage: int32 [4, 64, 64], P('vis', 'row', 'col'), may hold values from 0 to 1, as said below
- conv_one: float32 [32, 3, 3], replicated, may hold values from -2 to 2
- bias_one: float32 [32], replicated, may hold values from -3 to 3
- conv_two: bfloat16 [3, 3, 32, 32], replicated, may hold values from -0.375 to 0.375
- bias_two: float32 [32], replicated, may hold values from -3 to 3
Outputs:
- features: bfloat16 [32, 4096, 4096], P(None, ('vis', 'row', 'col'))
Inputs may be any that keep to these rules, and one draw needn't show every extreme that they name: `coverage`: 0 or 1; blocks near the grid's centre are touched by more groups than those near its corners.
All inputs are finite; a program needn't handle non-finite values.
Results may differ from a plain program's by a relative error of at most 0.014.
Values may be sent and summed in bfloat16 or wider, within the bound.
A program may use at most 64 MiB of HBM per device.

v0:
```python
import math

import jax
import jax.numpy as jnp
from jax import lax
from jax.sharding import PartitionSpec as P

BLK = 128


def with_halo(cells, sides, width):
    for axis, dim in sides:
        count = lax.axis_size(axis)
        ends = count - 1
        head = lax.slice_in_dim(cells, 0, width, axis=dim)
        tail = lax.slice_in_dim(cells, cells.shape[dim] - width, cells.shape[dim], axis=dim)
        cells = jnp.concatenate(
            [
                lax.ppermute(tail, axis, [(i, (i + 1) % count) for i in range(ends)]),
                cells,
                lax.ppermute(head, axis, [((i + 1) % count, i) for i in range(ends)]),
            ],
            axis=dim,
        )
    return cells


def phase_table(numer, denom):
    angle = numer.astype(jnp.float32) * (2.0 * math.pi / denom)
    return (jnp.cos(angle), jnp.sin(angle))


def partial_transform(real_part, imag_part, block_of, keep_imag):
    batch = real_part.shape[0]
    count_blocks = real_part.shape[1]
    block_len = real_part.shape[2]
    length = count_blocks * block_len
    highest = lax.Precision.HIGHEST
    outer = jnp.arange(count_blocks, dtype=jnp.int32)
    inner = jnp.arange(block_len, dtype=jnp.int32)
    cos_one, sin_one = phase_table(block_of[:, None] * outer[None, :] % count_blocks, count_blocks)
    mid_re = jnp.einsum("lpt,px->lxt", real_part, cos_one, precision=highest) - jnp.einsum(
        "lpt,px->lxt", imag_part, sin_one, precision=highest
    )
    mid_im = jnp.einsum("lpt,px->lxt", real_part, sin_one, precision=highest) + jnp.einsum(
        "lpt,px->lxt", imag_part, cos_one, precision=highest
    )
    cos_two, sin_two = phase_table(outer[:, None] * inner[None, :] % length, length)
    parity = (1 - 2 * (outer % 2)).astype(jnp.float32)[:, None]
    cos_two = cos_two * parity
    sin_two = sin_two * parity
    turn_re = mid_re * cos_two - mid_im * sin_two
    turn_im = mid_re * sin_two + mid_im * cos_two
    kept = jnp.arange(block_len // 2, dtype=jnp.int32)
    picked = (kept + 3 * block_len // 4) % block_len
    cos_three, sin_three = phase_table(inner[:, None] * picked[None, :] % block_len, block_len)
    out_re = jnp.einsum("lxt,tj->ljx", turn_re, cos_three, precision=highest) - jnp.einsum(
        "lxt,tj->ljx", turn_im, sin_three, precision=highest
    )
    out_re = out_re.reshape(batch, length // 2)
    if keep_imag:
        out_im = jnp.einsum("lxt,tj->ljx", turn_re, sin_three, precision=highest) + jnp.einsum(
            "lxt,tj->ljx", turn_im, cos_three, precision=highest
        )
        return (out_re, out_im.reshape(batch, length // 2))
    return (out_re, out_re)


def first_layer(extended, conv_one, bias_one, count_rows):
    width = extended.shape[1]
    padded = jnp.pad(extended, ((0, 0), (1, 1)))
    summed = (
        jnp.zeros((conv_one.shape[0], count_rows, width), jnp.float32) + bias_one[:, None, None]
    )
    for shift_b in range(3):
        for shift_a in range(3):
            summed = (
                summed
                + conv_one[:, shift_b, shift_a][:, None, None]
                * padded[None, shift_b : shift_b + count_rows, shift_a : shift_a + width]
            )
    return jnp.maximum(summed, 0.0)


def second_layer(hidden_ext, conv_two, bias_two, count_rows):
    width = hidden_ext.shape[2]
    padded = jnp.pad(hidden_ext, ((0, 0), (0, 0), (1, 1)))
    summed = jnp.zeros((conv_two.shape[2], count_rows, width), jnp.float32)
    for shift_b in range(3):
        for shift_a in range(3):
            summed = summed + jnp.einsum(
                "kj,jba->kba",
                conv_two[shift_b, shift_a],
                padded[:, shift_b : shift_b + count_rows, shift_a : shift_a + width],
                preferred_element_type=jnp.float32,
            )
    return (summed + bias_two[:, None, None]).astype(jnp.bfloat16)


def local(partials, coverage, conv_one, bias_one, conv_two, bias_two):
    count_vis = lax.axis_size("vis")
    count_row = lax.axis_size("row")
    count_col = lax.axis_size("col")
    grid_len = partials.shape[3] * count_col
    cover = coverage[0]
    block_rows = cover.shape[0]
    block_cols = cover.shape[1]
    spread = jnp.broadcast_to(cover[:, None, :, None], (block_rows, BLK, block_cols, BLK))
    spread = spread.reshape(block_rows * BLK, block_cols * BLK)
    count_blocks = count_vis * count_row
    row_block = grid_len // count_blocks
    row_share = row_block // count_col
    masked = partials[0] * spread.astype(jnp.bfloat16)[None]
    reduced = lax.psum_scatter(
        masked.astype(jnp.float32).astype(jnp.bfloat16), "vis", scatter_dimension=1, tiled=True
    ).astype(jnp.float32)
    grid_rows = lax.all_to_all(
        reduced.astype(jnp.bfloat16), "col", split_axis=1, concat_axis=2, tiled=True
    ).astype(reduced.dtype)
    natural = jnp.arange(count_blocks, dtype=jnp.int32)
    shaped = grid_rows.reshape(2, row_share, count_blocks, row_block)
    first_re, first_im = partial_transform(shaped[0], shaped[1], natural, True)
    stacked = jnp.stack([first_re, first_im])
    moved = lax.all_to_all(
        lax.all_to_all(
            stacked.astype(jnp.bfloat16), ("vis", "row"), split_axis=2, concat_axis=1, tiled=True
        ),
        "col",
        split_axis=2,
        concat_axis=1,
        tiled=True,
    ).astype(stacked.dtype)
    img_rows = moved.shape[2]
    arranged = moved.reshape(2, count_col, count_blocks, row_share, img_rows)
    arranged = arranged.transpose(0, 4, 2, 1, 3).reshape(2, img_rows, count_blocks, row_block)
    owners = natural % count_row * count_vis + natural // count_row
    image, unused = partial_transform(arranged[0], arranged[1], owners, False)
    image = image * (1.0 / grid_len)
    extended = with_halo(image.astype(jnp.bfloat16), ((("vis", "row", "col"), 0),), 1).astype(
        image.dtype
    )
    hidden = first_layer(extended, conv_one, bias_one, img_rows).astype(jnp.bfloat16)
    hidden_ext = with_halo(hidden, ((("vis", "row", "col"), 1),), 1)
    return second_layer(hidden_ext, conv_two, bias_two, img_rows)


def solution(mesh):
    placed = (P("vis", None, "row", "col"), P("vis", "row", "col"), P(), P(), P(), P())
    return jax.shard_map(
        local,
        mesh=mesh,
        in_specs=placed,
        out_specs=P(None, ("vis", "row", "col"), None),
        check_vma=False,
    )
```

profile of v0, /device:TPU:1, one launch (start us, length us, event | category | flops | bytes accessed | tf_op | source)
XLA Modules:
  0.0 239.5 jit_solution(2143959087701187884)
XLA Ops:
  8.1 4.4 %bitcast_multiply_fusion = bf16[2,512,1024]{2,0,1:T(2,128)(2,1)} fusion(bf16[1,2,512,1024]{3,2,1,0:T(8,128)(2,1)S(1)} %copy-done, bf16[512,1024]{1,0:T(8,128)(2,1)S(1)} %bitcast.169), kind=kLoop, calls=%fused_computation.32 | loop fusion | flops 1048576 | bytes 5242880 | tf_op jit(solution)/shard_map/mul | solution.py:113
  14.4 76.7 %all-reduce.5.cloned.1.call-done = bf16[2,512,1024]{2,0,1:T(2,128)(2,1)} async-done(((bf16[2,512,1024]{2,0,1:T(2,128)(2,1)}), bf16[2,512,1024]{2,0,1:T(2,128)(2,1)}) %all-reduce.5.cloned.1.call-update) | async-done | bytes 2097168
  91.1 2.2 constant_dynamic-slice_fusion
  93.3 6.1 %all-to-all-start = ((bf16[2,128,1024]{2,0,1:T(2,128)(2,1)}), bf16[2,128,1024]{2,0,1:T(2,128)(2,1)S(1)}, u32[]{:S(2)}, u32[]{:S(2)}) async-start(bf16[2,128,1024]{2,0,1:T(2,128)(2,1)} %constant_dynamic-slice_fusion), calls=%async_computation | async-start | bytes 1048576 | tf_op jit(solution)/shard_map/all_to_all | solution.py:117
  99.6 11.6 %all-to-all-done = bf16[2,128,1024]{2,0,1:T(2,128)(2,1)S(1)} async-done(((bf16[2,128,1024]{2,0,1:T(2,128)(2,1)}), bf16[2,128,1024]{2,0,1:T(2,128)(2,1)S(1)}, u32[]{:S(2)}, u32[]{:S(2)}) %all-to-all-start) | async-done | bytes 524320 | tf_op jit(solution)/shard_map/all_to_all | solution.py:117
  113.7 1.8 fusion.29
  115.5 1.8 fusion.31
  117.3 1.8 fusion.22
  119.4 1.8 fusion.23
  121.5 2.7 %copy.45 = bf16[2,16,4096]{1,0,2:T(2,128)(2,1)S(1)} copy(bf16[2,16,4096]{2,1,0:T(8,128)(2,1)S(1)} %pad_maximum_fusion.4) | data formatting | bytes 524288 | tf_op jit(solution)/shard_map/stack | solution.py:123
  124.3 2.3 reshape.169
  126.6 33.9 %all_to_all.48 = bf16[64,2,1024]{2,1,0:T(2,128)(2,1)S(1)} all-to-all(bf16[64,2,1024]{2,1,0:T(2,128)(2,1)S(1)} %reshape.169), channel_id=1, replica_groups=mesh['vis'=4,'row'=16,'col'=8] {'vis','row'}, dimensions={0} | all-to-all | bytes 524288 | tf_op jit(solution)/shard_map/all_to_all | solution.py:125
  161.9 2.4 copy.62
  165.2 3.4 %all-to-all-start.2 = ((bf16[2,1024,64]{1,0,2:T(2,128)(2,1)}), bf16[2,1024,64]{1,0,2:T(2,128)(2,1)S(1)}, u32[]{:S(2)}, u32[]{:S(2)}) async-start(bf16[2,1024,64]{1,0,2:T(2,128)(2,1)} %copy.48), calls=%async_computation.2 | async-start | bytes 524288 | tf_op jit(solution)/shard_map/all_to_all | solution.py:124
  168.7 7.7 %all-to-all-done.2 = bf16[2,1024,64]{1,0,2:T(2,128)(2,1)S(1)} async-done(((bf16[2,1024,64]{1,0,2:T(2,128)(2,1)}), bf16[2,1024,64]{1,0,2:T(2,128)(2,1)S(1)}, u32[]{:S(2)}, u32[]{:S(2)}) %all-to-all-start.2) | async-done | bytes 262176 | tf_op jit(solution)/shard_map/all_to_all | solution.py:124
  185.5 4.3 %collective-permute-start.1 = (bf16[1,4096]{1,0:T(2,128)(2,1)S(1)}, bf16[1,4096]{1,0:T(2,128)(2,1)S(1)}, u32[]{:S(2)}, u32[]{:S(2)}) collective-permute-start(bf16[1,4096]{1,0:T(2,128)(2,1)S(1)} %slice.156), channel_id=1, source_target_pairs={{1,0},{2,1},{3,2},{4,3},{5,4},{6,5},{7,6},{8,7},{9,8},{10,9},{11,1... | collective-permute-start | bytes 24584 | tf_op jit(solution)/shard_map/ppermute | solution.py:21
  189.9 1.9 collective-permute-start
  192.0 8.6 %collective-permute-done = bf16[1,4096]{1,0:T(2,128)(2,1)S(1)} collective-permute-done((bf16[1,4096]{1,0:T(2,128)(2,1)S(1)}, bf16[1,4096]{1,0:T(2,128)(2,1)S(1)}, u32[]{:S(2)}, u32[]{:S(2)}) %collective-permute-start) | collective-permute-done | bytes 8224 | tf_op jit(solution)/shard_map/ppermute | solution.py:19
  201.0 3.1 %maximum_convert_fusion = bf16[32,8,4096]{2,0,1:T(8,128)(2,1)S(1)} fusion(f32[8,4096]{1,0:T(8,128)S(1)} %get-tuple-element.16, f32[32]{0:T(128)S(1)} %get-tuple-element.29, f32[8,4096]{1,0:T(8,128)S(1)} %get-tuple-element.17, f32[32]{0:T(128)S(1)} %get-tuple-element.30, f32[8,4096]{1,0:T(8,128)S(1)} %get-tuple-element.15, f32[32]{0:T(128)S(1)} %get-tuple-element.23, ...), kind=kLoop, calls=%fused_computation.14 | loop fusion | flops 20971520 | bytes 3278080 | tf_op jit(solution)/shard_map/convert_element_type | solution.py:142
  204.1 1.9 collective-permute-start.2
  206.1 9.6 %collective-permute-start.3 = (bf16[32,1,4096]{2,0,1:T(8,128)(2,1)S(1)}, bf16[32,1,4096]{2,0,1:T(8,128)(2,1)S(1)}, u32[]{:S(2)}, u32[]{:S(2)}) collective-permute-start(bf16[32,1,4096]{2,0,1:T(8,128)(2,1)S(1)} %get-tuple-element.6), channel_id=1, source_target_pairs={{1,0},{2,1},{3,2},{4,3},{5,4},{6,5},{7,6},{8,7},{9,8},{10,9},{11,1... | collective-permute-start | bytes 786440 | tf_op jit(solution)/shard_map/ppermute | solution.py:21
  215.7 2.9 %collective-permute-done.2 = bf16[32,1,4096]{2,0,1:T(8,128)(2,1)S(1)} collective-permute-done((bf16[32,1,4096]{2,0,1:T(8,128)(2,1)S(1)}, bf16[32,1,4096]{2,0,1:T(8,128)(2,1)S(1)}, u32[]{:S(2)}, u32[]{:S(2)}) %collective-permute-start.2) | collective-permute-done | bytes 262176 | tf_op jit(solution)/shard_map/ppermute | solution.py:19
  224.1 3.7 %convolution_add_fusion.3 = f32[8,4096,32]{1,2,0:T(8,128)S(1)} fusion(f32[8,4096,32]{1,2,0:T(8,128)S(1)} %convolution_add_fusion.4, bf16[3,3,32,32]{3,2,1,0:T(8,128)(2,1)S(1)} %copy-done.1, f32[8,4096]{1,0:T(8,128)S(1)} %get-tuple-element.16, f32[32]{0:T(128)S(1)} %get-tuple-element.29, f32[8,4096]{1,0:T(8,128)S(1)} %get-tuple-element.17, ...), kind=kOutput, calls=%fused_computation.5 | convolution fusion | flops 89128960 | bytes 9581568 | tf_op jit(solution)/shard_map/kj,jba->kba/dot_general | solution.py:91
  230.2 2.5 %copy.56 = bf16[32,8,4096]{2,1,0:T(8,128)(2,1)} copy(bf16[32,8,4096]{2,0,1:T(8,128)(2,1)S(1)} %fusion.4) | data formatting | bytes 4194304 | tf_op jit(solution)/shard_map/convert_element_type | solution.py:97
  (63 shorter events, 26.0 us)
Async XLA Ops:
  6.5 1.6 copy-start
  6.5 84.6 %all-reduce.5.cloned.1.call-start = ((), (), s32[]{:S(2)}) async-start(), calls=%async_computation.3 | async-start | bytes 4194304
  93.3 17.9 %all-to-all-start = ((bf16[2,128,1024]{2,0,1:T(2,128)(2,1)}), bf16[2,128,1024]{2,0,1:T(2,128)(2,1)S(1)}, u32[]{:S(2)}, u32[]{:S(2)}) async-start(bf16[2,128,1024]{2,0,1:T(2,128)(2,1)} %constant_dynamic-slice_fusion), calls=%async_computation | async-start | bytes 1048576 | tf_op jit(solution)/shard_map/all_to_all | solution.py:117
  165.2 11.1 %all-to-all-start.2 = ((bf16[2,1024,64]{1,0,2:T(2,128)(2,1)}), bf16[2,1024,64]{1,0,2:T(2,128)(2,1)S(1)}, u32[]{:S(2)}, u32[]{:S(2)}) async-start(bf16[2,1024,64]{1,0,2:T(2,128)(2,1)} %copy.48), calls=%async_computation.2 | async-start | bytes 524288 | tf_op jit(solution)/shard_map/all_to_all | solution.py:124
  179.3 12.5 %copy-start.2 = (f32[32,3,3]{0,2,1:T(4,128)S(1)}, f32[32,3,3]{0,2,1:T(4,128)}, u32[]{:S(2)}) copy-start(f32[32,3,3]{0,2,1:T(4,128)} %param.8) | copy-start | bytes 3460
  180.9 20.1 %copy-start.3 = (f32[32]{0:T(128)S(1)}, f32[32]{0:T(128)}, u32[]{:S(2)}) copy-start(f32[32]{0:T(128)} %param.9) | copy-start | bytes 388
  185.5 6.5 %collective-permute-start.1 = (bf16[1,4096]{1,0:T(2,128)(2,1)S(1)}, bf16[1,4096]{1,0:T(2,128)(2,1)S(1)}, u32[]{:S(2)}, u32[]{:S(2)}) collective-permute-start(bf16[1,4096]{1,0:T(2,128)(2,1)S(1)} %slice.156), channel_id=1, source_target_pairs={{1,0},{2,1},{3,2},{4,3},{5,4},{6,5},{7,6},{8,7},{9,8},{10,9},{11,1... | collective-permute-start | bytes 24584 | tf_op jit(solution)/shard_map/ppermute | solution.py:21
  189.9 10.8 %collective-permute-start = (bf16[1,4096]{1,0:T(2,128)(2,1)S(1)}, bf16[1,4096]{1,0:T(2,128)(2,1)S(1)}, u32[]{:S(2)}, u32[]{:S(2)}) collective-permute-start(bf16[1,4096]{1,0:T(2,128)(2,1)S(1)} %slice.154), channel_id=1, source_target_pairs={{0,1},{1,2},{2,3},{3,4},{4,5},{5,6},{6,7},{7,8},{8,9},{9,10},{10,1... | collective-permute-start | bytes 24584 | tf_op jit(solution)/shard_map/ppermute | solution.py:19
  201.0 19.3 %copy-start.1 = (bf16[3,3,32,32]{3,2,1,0:T(8,128)(2,1)S(1)}, bf16[3,3,32,32]{3,2,1,0:T(8,128)(2,1)}, u32[]{:S(2)}) copy-start(bf16[3,3,32,32]{3,2,1,0:T(8,128)(2,1)} %param.10) | copy-start | bytes 55300
  204.1 14.5 %collective-permute-start.2 = (bf16[32,1,4096]{2,0,1:T(8,128)(2,1)S(1)}, bf16[32,1,4096]{2,0,1:T(8,128)(2,1)S(1)}, u32[]{:S(2)}, u32[]{:S(2)}) collective-permute-start(bf16[32,1,4096]{2,0,1:T(8,128)(2,1)S(1)} %get-tuple-element.5), channel_id=1, source_target_pairs={{0,1},{1,2},{2,3},{3,4},{4,5},{5,6},{6,7},{7,8},{8,9},{9,10},{10,1... | collective-permute-start | bytes 786440 | tf_op jit(solution)/shard_map/ppermute | solution.py:19
  206.1 12.7 %collective-permute-start.3 = (bf16[32,1,4096]{2,0,1:T(8,128)(2,1)S(1)}, bf16[32,1,4096]{2,0,1:T(8,128)(2,1)S(1)}, u32[]{:S(2)}, u32[]{:S(2)}) collective-permute-start(bf16[32,1,4096]{2,0,1:T(8,128)(2,1)S(1)} %get-tuple-element.6), channel_id=1, source_target_pairs={{1,0},{2,1},{3,2},{4,3},{5,4},{6,5},{7,6},{8,7},{9,8},{10,9},{11,1... | collective-permute-start | bytes 786440 | tf_op jit(solution)/shard_map/ppermute | solution.py:21
  228.7 0.8 copy-start.4
Sparse Core Ops, SparseCore 0:
  12.7 78.3 all-reduce.4
where the time goes:
time: 242 us; the launch traced here: 240 us
  waiting for transfers between devices  108 us (45%)
  blocking collectives  33.9 us (14%)
  starting transfers between devices  27.3 us (11%)
  local copies, waits for them, and re-layouts  23.2 us (10%)
  matrix products  23 us (10%)
  between operations  14.3 us (6%)
  other arithmetic  10.2 us (4%)
    unnamed x2, waiting for transfers between devices  76.7 us
    all_to_all x1, blocking collectives, local(): lax.all_to_all(stacked.astype(jnp.bfloat16), ('vis', 'row'), split_axis=2...  33.9 us
    ppermute x2, starting transfers between devices, with_halo(): lax.ppermute(head, axis, [((i + 1) % count, i) for i in range(ends)])  13.9 us
    ppermute x2, waiting for transfers between devices, with_halo(): lax.ppermute(tail, axis, [(i, (i + 1) % count) for i in range(ends)])  11.6 us
    all_to_all x1, waiting for transfers between devices, local(): lax.all_to_all(reduced.astype(jnp.bfloat16), 'col', split_axis=1, concat_...  11.6 us
    dot_general x9, matrix products, second_layer(): jnp.einsum('kj,jba->kba', conv_two[shift_b, shift_a], padded[:, shift_b:s...  9.79 us
    unnamed x15, local copies, waits for them, and re-layouts  7.73 us
    all_to_all x1, waiting for transfers between devices, local(): lax.all_to_all(lax.all_to_all(stacked.astype(jnp.bfloat16), ('vis', 'row'...  7.66 us
  transfers between devices with their start and end apart: 7, of which 6 were waited for; matrix products, arithmetic and copies ran while one was open for 1% of the time, Pallas kernels for 0%

commit v1 on v0

v1 whole, which is shorter than its diff:
```python
import functools

import jax
import jax.numpy as jnp
import numpy as np
from jax import lax
from jax.experimental import pallas as pl
from jax.experimental.pallas import tpu as pltpu
from jax.sharding import PartitionSpec as P

MESH = pl.DeviceIdType.MESH
F32 = jnp.float32
BF16 = jnp.bfloat16
N = 8192
CHIP_ORDER = (
    (1, 0), (3, 0), (0, 1), (0, 3), (1, 1), (3, 3), (1, 3), (3, 1),
    (2, 0), (0, 2), (2, 1), (1, 2), (2, 3), (3, 2), (2, 2),
)
Z_ORDER = (8, 7, 9, 6, 10, 5, 11, 4, 12, 3, 13, 2, 14, 1, 15)


def tables():
    p = np.arange(1024)
    tw1 = np.zeros((16, 1024))
    for beta in range(8):
        ang = 2 * np.pi * p * beta / N
        tw1[2 * beta] = (-1) ** beta * np.cos(ang)
        tw1[2 * beta + 1] = (-1) ** beta * np.sin(ang)
    l = np.arange(128)
    mat = np.zeros((8, 4, 2, 16, 256))
    for bp in range(8):
        idx = np.arange(64).reshape(4, 16)
        ang = 2 * np.pi * l * (8 * (idx[..., None] - 32) + bp) / 1024
        mat[bp, :, 0, :, :128] = np.cos(ang)
        mat[bp, :, 0, :, 128:] = -np.sin(ang)
        mat[bp, :, 1, :, :128] = np.sin(ang)
        mat[bp, :, 1, :, 128:] = np.cos(ang)
    k = np.arange(512)
    ang = 2 * np.pi * ((k[:, None] * k[None, :]) % 512) / 512
    cs = np.concatenate([np.cos(ang), np.sin(ang)], axis=1)
    tt = np.arange(16)
    ang = 2 * np.pi * tt[:, None] * k[None, :] / N
    sign = (1 - 2 * (k % 2)) / N
    tw2 = np.stack([np.cos(ang) * sign, np.sin(ang) * sign], axis=1).reshape(32, 512)
    return (
        jnp.asarray(tw1, F32),
        jnp.asarray(mat.reshape(8, 128, 256), BF16),
        jnp.asarray(cs, BF16),
        jnp.asarray(tw2, F32),
    )


def add(a, b):
    return (a[0] + b[0], a[1] + b[1])


def sub(a, b):
    return (a[0] - b[0], a[1] - b[1])


def add_i(a, b):
    return (a[0] - b[1], a[1] + b[0])


def sub_i(a, b):
    return (a[0] + b[1], a[1] - b[0])


def dft8(x):
    r = 0.5**0.5
    a0, a1, a2, a3 = add(x[0], x[4]), sub(x[0], x[4]), add(x[2], x[6]), sub(x[2], x[6])
    o0, o1, o2, o3 = add(x[1], x[5]), sub(x[1], x[5]), add(x[3], x[7]), sub(x[3], x[7])
    even = [add(a0, a2), add_i(a1, a3), sub(a0, a2), sub_i(a1, a3)]
    odd = [add(o0, o2), add_i(o1, o3), sub(o0, o2), sub_i(o1, o3)]
    w1 = ((odd[1][0] - odd[1][1]) * r, (odd[1][0] + odd[1][1]) * r)
    w3 = ((-odd[3][0] - odd[3][1]) * r, (odd[3][0] - odd[3][1]) * r)
    return [
        add(even[0], odd[0]), add(even[1], w1), add_i(even[2], odd[2]), add(even[3], w3),
        sub(even[0], odd[0]), sub(even[1], w1), sub_i(even[2], odd[2]), sub(even[3], w3),
    ]


def image_kernel(
    part, cover, tw1_h, mat_h, cs_h, tw2_h,
    image, halo,
    xin, pair_out, pair_in, rows_out, rows_in, mid, spec, slab_out, slab_in, slab_f, z_out, z_in, acc,
    halo_out, tw1, mat, cs, tw2,
    sem_in, sem_tab, ps, pr, cs_s, cr, ss, sr, zs, zr, hs, hr,
):
    vis = lax.axis_index("vis")
    row = lax.axis_index("row")
    col = lax.axis_index("col")
    core = vis % 2
    ylo = vis // 2
    x = col % 4
    y = (col // 4) * 2 + ylo
    chip = ylo * 8 + col
    mine = core * 16 + chip
    linear = vis * 128 + row * 8 + col

    def at(v, r, c):
        return {"vis": v, "row": r, "col": c}

    def chip_of(dx, dy):
        xx, yy = (x + dx) % 4, (y + dy) % 4
        return yy % 2, (yy // 2) * 4 + xx

    def neighbour(step):
        n = (linear + step) % 512
        return at(n // 128, (n // 8) % 16, n % 8)

    partner = at(vis + 1 - 2 * core, row, col)
    chips = [chip_of(dx, dy) for dx, dy in CHIP_ORDER]
    slab = [partner]
    for cy, cc in chips:
        slab.append(at(cy * 2 + core, row, cc))
        slab.append(at(cy * 2 + 1 - core, row, cc))
    depth = [at(vis, (row + dz) % 16, col) for dz in Z_ORDER]
    after, before = neighbour(1), neighbour(511)

    barrier = pltpu.get_barrier_semaphore()
    for peer in depth + slab + [after, before]:
        pl.semaphore_signal(barrier, inc=1, device_id=peer, device_id_type=MESH)

    def rows_of(half, blk):
        return pl.ds(pl.multiple_of(half * 256 + blk * 128, 128), 128)

    loads = []
    for h, half in enumerate((1 - core, core)):
        for blk in range(2):
            for ri in range(2):
                slot = h * 4 + blk * 2 + ri
                c = pltpu.make_async_copy(
                    part.at[ri, rows_of(half, blk)], xin.at[slot], sem_in.at[slot]
                )
                c.start()
                loads.append(c)
    tabs = [
        pltpu.make_async_copy(src, dst, sem_tab.at[i])
        for i, (src, dst) in enumerate(((tw1_h, tw1), (mat_h, mat), (cs_h, cs), (tw2_h, tw2)))
    ]
    for c in tabs:
        c.start()
    pl.semaphore_wait(barrier, len(depth) + len(slab) + 2)

    def masked(slot, half, blk, dst, dslot):
        def one(j, carry):
            lanes = pl.ds(pl.multiple_of(j * 128, 128), 128)
            m = jnp.full((128, 128), cover[half * 2 + blk, j].astype(F32)).astype(BF16)
            dst[dslot, :, lanes] = xin[slot, :, lanes] * m
            return carry

        lax.fori_loop(0, 8, one, 0)

    sends = []
    for blk in range(2):
        for ri in range(2):
            slot = blk * 2 + ri
            loads[slot].wait()
            masked(slot, 1 - core, blk, pair_out, slot)
            c = pltpu.make_async_remote_copy(
                src_ref=pair_out.at[slot],
                dst_ref=pair_in.at[slot],
                send_sem=ps.at[slot],
                recv_sem=pr.at[slot],
                device_id=partner,
                device_id_type=MESH,
            )
            c.start()
            sends.append(c)
    for blk in range(2):
        for ri in range(2):
            slot = blk * 2 + ri
            loads[4 + slot].wait()
            masked(4 + slot, core, blk, xin, 4 + slot)
    for blk in range(2):
        for ri in range(2):
            slot = blk * 2 + ri
            sends[slot].wait_recv()

            def one(i, carry):
                r = pl.ds(pl.multiple_of(i * 16, 16), 16)
                s = xin[4 + slot, r, :].astype(F32) + pair_in[slot, r, :].astype(F32)
                rows_out[blk * 8 + i, ri] = s.astype(BF16)
                return carry

            lax.fori_loop(0, 8, one, 0)

    chip_sends = []
    for i, (cy, cc) in enumerate(chips):
        c = pltpu.make_async_remote_copy(
            src_ref=rows_out.at[cy * 8 + cc],
            dst_ref=rows_in.at[chip],
            send_sem=cs_s.at[i],
            recv_sem=cr.at[i],
            device_id=at(cy * 2 + core, row, cc),
            device_id_type=MESH,
        )
        c.start()
        chip_sends.append(c)
    rows_in[chip] = rows_out[chip]
    for c in sends:
        c.wait_send()
    for c in tabs:
        c.wait()
    for c in chip_sends:
        c.wait_recv()

    def stage_one(q, carry):
        lanes = pl.ds(pl.multiple_of(q * 128, 128), 128)
        xs = []
        for c in range(8):
            xs.append(
                tuple(
                    rows_in[c, ri, :, lanes].astype(F32) + rows_in[8 + c, ri, :, lanes].astype(F32)
                    for ri in range(2)
                )
            )
        for beta, (re, im) in enumerate(dft8(xs)):
            wr = jnp.broadcast_to(tw1[2 * beta : 2 * beta + 1, lanes], (16, 128))
            wi = jnp.broadcast_to(tw1[2 * beta + 1 : 2 * beta + 2, lanes], (16, 128))
            mid[beta, q, 0] = re * wr - im * wi
            mid[beta, q, 1] = re * wi + im * wr
        return carry

    lax.fori_loop(0, 8, stage_one, 0)

    def stage_two(beta, carry):
        rows = pl.ds(pl.multiple_of(beta * 16, 16), 16)
        xs = [(mid[beta, q, 0], mid[beta, q, 1]) for q in range(8)]
        for bp, (re, im) in enumerate(dft8(xs)):
            spec[bp, rows, 0:128] = re.astype(BF16)
            spec[bp, rows, 128:256] = im.astype(BF16)
        return carry

    lax.fori_loop(0, 8, stage_two, 0)

    def stage_three(bp, carry):
        out = lax.dot_general(
            mat[bp], spec[bp], (((1,), (1,)), ((), ())), preferred_element_type=F32
        ).astype(BF16)
        for v in range(4):
            slab_out[v * 8 + bp] = out[v * 32 : (v + 1) * 32]
        return carry

    lax.fori_loop(0, 8, stage_three, 0)

    slab_sends = []
    places = []
    for cy, cc in chips:
        places.append((cy * 2 + core, cc))
        places.append((cy * 2 + 1 - core, cc))
    places.append((vis + 1 - 2 * core, col))
    for i, (v, c_) in enumerate(places):
        c = pltpu.make_async_remote_copy(
            src_ref=slab_out.at[v * 8 + c_],
            dst_ref=slab_in.at[mine],
            send_sem=ss.at[i],
            recv_sem=sr.at[i],
            device_id=at(v, row, c_),
            device_id_type=MESH,
        )
        c.start()
        slab_sends.append(c)
    slab_in[mine] = slab_out[vis * 8 + col]
    for c in chip_sends:
        c.wait_send()
    for c in slab_sends:
        c.wait_recv()

    def widen(d, carry):
        slab_f[pl.ds(pl.multiple_of(d * 32, 32), 32), :] = slab_in[d].astype(F32)
        return carry

    lax.fori_loop(0, 32, widen, 0)
    for z in range(16):
        z_out[z, :, 0:128] = slab_f[pl.ds(z, 32, stride=32), :].astype(BF16)
        z_out[z, :, 128:256] = slab_f[pl.ds(16 + z, 32, stride=32), :].astype(BF16)
    z_sends = []
    for i, dz in enumerate(Z_ORDER):
        c = pltpu.make_async_remote_copy(
            src_ref=z_out.at[(row + dz) % 16],
            dst_ref=z_in.at[row],
            send_sem=zs.at[i],
            recv_sem=zr.at[i],
            device_id=depth[i],
            device_id_type=MESH,
        )
        c.start()
        z_sends.append(c)
    z_in[row] = z_out[row]
    for c in slab_sends:
        c.wait_send()
    for c in z_sends:
        c.wait_recv()

    out = lax.dot_general(
        z_in[...].reshape(512, 256), cs[...], (((0,), (0,)), ((), ())), preferred_element_type=F32
    )
    for i in range(8):
        acc[i] = out[:, i * 128 : (i + 1) * 128]

    def last(q, carry):
        lo = pl.ds(pl.multiple_of(q * 128, 128), 128)
        vs = []
        for tt in range(16):
            top, bot = pl.ds(tt, 8, stride=16), pl.ds(128 + tt, 8, stride=16)
            re = acc[q, top, :] - acc[4 + q, bot, :]
            im = acc[4 + q, top, :] + acc[q, bot, :]
            wr = jnp.broadcast_to(tw2[2 * tt : 2 * tt + 1, lo], (8, 128))
            wi = jnp.broadcast_to(tw2[2 * tt + 1 : 2 * tt + 2, lo], (8, 128))
            vs.append((re * wr - im * wi, re * wi + im * wr))
        even = dft8([add(vs[t], vs[t + 8]) for t in range(8)])
        turned = []
        for t in range(8):
            a, b = float(np.cos(np.pi * t / 8)), float(np.sin(np.pi * t / 8))
            re, im = sub(vs[t], vs[t + 8])
            turned.append((re * a - im * b, re * b + im * a))
        odd = dft8(turned)
        for i, k in enumerate((6, 7, 0, 1)):
            image[:, pl.ds(pl.multiple_of((2 * i) * 512 + q * 128, 128), 128)] = even[k][0]
            image[:, pl.ds(pl.multiple_of((2 * i + 1) * 512 + q * 128, 128), 128)] = odd[k][0]
        return carry

    lax.fori_loop(0, 4, last, 0)

    for i in range(2):
        for j in range(4):
            lanes = slice(j * 1024, (j + 1) * 1024)
            halo_out[0, i * 4 + j : i * 4 + j + 1, :] = image[i : i + 1, lanes]
            halo_out[1, i * 4 + j : i * 4 + j + 1, :] = image[6 + i : 7 + i, lanes]
    halo_sends = []
    for i, peer in enumerate((before, after)):
        c = pltpu.make_async_remote_copy(
            src_ref=halo_out.at[i],
            dst_ref=halo.at[1 - i],
            send_sem=hs.at[i],
            recv_sem=hr.at[i],
            device_id=peer,
            device_id_type=MESH,
        )
        c.start()
        halo_sends.append(c)
    for c in z_sends:
        c.wait_send()
    for c in halo_sends:
        c.wait()


def image_rows(partials, coverage):
    any_spec = pl.BlockSpec(memory_space=pl.ANY)
    vmem = pl.BlockSpec(memory_space=pltpu.VMEM)
    dma = pltpu.SemaphoreType.DMA
    return pl.pallas_call(
        image_kernel,
        out_shape=(
            jax.ShapeDtypeStruct((8, 4096), F32),
            jax.ShapeDtypeStruct((2, 8, 1024), F32),
        ),
        in_specs=[any_spec, pl.BlockSpec(memory_space=pltpu.SMEM)] + [any_spec] * 4,
        out_specs=(vmem, vmem),
        scratch_shapes=[
            pltpu.VMEM((8, 128, 1024), BF16),
            pltpu.VMEM((4, 128, 1024), BF16),
            pltpu.VMEM((4, 128, 1024), BF16),
            pltpu.VMEM((16, 2, 16, 1024), BF16),
            pltpu.VMEM((16, 2, 16, 1024), BF16),
            pltpu.VMEM((8, 8, 2, 16, 128), F32),
            pltpu.VMEM((8, 128, 256), BF16),
            pltpu.VMEM((32, 32, 128), BF16),
            pltpu.VMEM((32, 32, 128), BF16),
            pltpu.VMEM((1024, 128), F32),
            pltpu.VMEM((16, 32, 256), BF16),
            pltpu.VMEM((16, 32, 256), BF16),
            pltpu.VMEM((8, 256, 128), F32),
            pltpu.VMEM((2, 8, 1024), F32),
            pltpu.VMEM((16, 1024), F32),
            pltpu.VMEM((8, 128, 256), BF16),
            pltpu.VMEM((512, 1024), BF16),
            pltpu.VMEM((32, 512), F32),
            dma((8,)), dma((4,)), dma((4,)), dma((4,)), dma((15,)), dma((15,)),
            dma((31,)), dma((31,)), dma((15,)), dma((15,)), dma((2,)), dma((2,)),
        ],
        name="image_rows",
        compiler_params=pltpu.CompilerParams(
            collective_id=0, has_side_effects=True, vmem_limit_bytes=40 * 2**20
        ),
    )(partials, coverage, *tables())


def conv_kernel(chunk, image, halo, w1, w2, b2, out, ext, shifted):
    ext[2:10, :] = image[...]
    for i in range(2):
        for j in range(4):
            lanes = slice(j * 1024, (j + 1) * 1024)
            ext[i : i + 1, lanes] = halo[0, i * 4 + j : i * 4 + j + 1, :]
            ext[10 + i : 11 + i, lanes] = halo[1, i * 4 + j : i * 4 + j + 1, :]
    width = image.shape[1]
    ext[12:16, :] = jnp.ones((4, width), F32)
    full = ext[...]
    lane = lax.broadcasted_iota(jnp.int32, full.shape, 1)
    for i, delta in enumerate(range(-2, 3)):
        if delta == 0:
            v = full
        else:
            v = pltpu.roll(full, (-delta) % width, 1)
            inside = (lane + delta >= 0) & (lane + delta < width)
            v = jnp.where(inside, v, 0.0)
        hi = v.astype(BF16)
        lo = (v - hi.astype(F32)).astype(BF16)
        shifted[i * 48 : i * 48 + 16, :] = hi
        shifted[i * 48 + 16 : i * 48 + 32, :] = lo
        shifted[i * 48 + 32 : i * 48 + 48, :] = hi

    def one(c, carry):
        lanes = pl.ds(pl.multiple_of(c * chunk, chunk), chunk)
        at = c * chunk + lax.broadcasted_iota(jnp.int32, (320, 128), 1)
        parts = []
        for s in range(3):
            h = jnp.dot(w1[...], shifted[s * 48 : s * 48 + 144, lanes], preferred_element_type=F32)
            h = jnp.maximum(h, 0.0)
            if s == 0:
                edge = jnp.where(at > 0, h[:, :128], 0.0)
                h = jnp.concatenate([edge, h[:, 128:]], axis=1)
            if s == 2:
                edge = jnp.where(at + (chunk - 128) < width - 1, h[:, chunk - 128 :], 0.0)
                h = jnp.concatenate([h[:, : chunk - 128], edge], axis=1)
            parts.append(h.astype(BF16))
        hidden = jnp.concatenate(parts, axis=0)
        o = jnp.dot(w2[...], hidden, preferred_element_type=F32) + b2[...]
        out[:, :, lanes] = o.reshape(32, 8, chunk).astype(BF16)
        return carry

    lax.fori_loop(0, width // chunk, one, 0)


def conv_weights(conv_one, bias_one, conv_two, bias_two):
    linear = lax.axis_index("vis") * 128 + lax.axis_index("row") * 8 + lax.axis_index("col")
    hr = jnp.arange(10)
    ir = jnp.arange(16)
    tap = (ir[None, :, None] == hr[:, None, None] + jnp.arange(3)[None, None, :]).astype(F32)
    w1 = jnp.einsum("hir,krs->hksi", tap, conv_one, precision=lax.Precision.HIGHEST)
    ones_row = ((ir[None, :] == 12) & (jnp.arange(3)[:, None] == 1)).astype(F32)
    w1 = w1 + bias_one[None, :, None, None] * ones_row[None, None]
    keep = ~(((hr == 0) & (linear == 0)) | ((hr == 9) & (linear == 511)))
    seen = ~(((ir < 2) & (linear == 0)) | ((ir // 2 == 5) & (linear == 511)))
    w1 = w1 * (keep[:, None] & seen[None, :]).astype(F32)[:, None, None, :]
    hi = w1.astype(BF16)
    lo = (w1 - hi.astype(F32)).astype(BF16)
    w1 = jnp.stack([hi, hi, lo], axis=3).reshape(320, 144)
    b = jnp.arange(8)
    tap2 = (hr[None, :, None] == b[:, None, None] + jnp.arange(3)[None, None, :]).astype(BF16)
    w2 = jnp.einsum("bhr,rskj->kbshj", tap2, conv_two, preferred_element_type=F32)
    w2 = w2.astype(BF16).reshape(256, 960)
    b2 = jnp.repeat(bias_two, 8)[:, None]
    return w1, w2, b2


def convolve(image, halo, conv_one, bias_one, conv_two, bias_two):
    chunk = 512
    w1, w2, b2 = conv_weights(conv_one, bias_one, conv_two, bias_two)
    vmem = pl.BlockSpec(memory_space=pltpu.VMEM)
    return pl.pallas_call(
        functools.partial(conv_kernel, chunk),
        out_shape=jax.ShapeDtypeStruct((32, 8, 4096), BF16),
        in_specs=[vmem] * 5,
        out_specs=vmem,
        scratch_shapes=[pltpu.VMEM((16, 4096), F32), pltpu.VMEM((240, 4096), BF16)],
        name="convolve",
        compiler_params=pltpu.CompilerParams(vmem_limit_bytes=40 * 2**20),
    )(image, halo, w1, w2, b2)


def local(partials, coverage, conv_one, bias_one, conv_two, bias_two):
    image, halo = image_rows(partials[0], coverage[0])
    return convolve(image, halo, conv_one, bias_one, conv_two, bias_two)


def solution(mesh):
    placed = (P("vis", None, "row", "col"), P("vis", "row", "col"), P(), P(), P(), P())
    return jax.shard_map(
        local,
        mesh=mesh,
        in_specs=placed,
        out_specs=P(None, ("vis", "row", "col"), None),
        check_vma=False,
    )
```

time: 242 us -> 89.5 us (0.37)
  waiting for transfers between devices: 108 us -> 0 us
  Pallas kernels: 0 us -> 74.6 us
  blocking collectives: 33.9 us -> 0 us
  starting transfers between devices: 27.3 us -> 0 us
  matrix products: 23 us -> 2.61 us
  between operations: 14.3 us -> 0.13 us
  local copies, waits for them, and re-layouts: 23.2 us -> 10.7 us
  other arithmetic: 10.2 us -> 1.15 us
    unnamed x2 -> x0, waiting for transfers between devices: 76.7 us -> none
    pallas_call x0 -> x2, Pallas kernels: none -> 74.6 us  [the longest x1 67.5 us: image_rows(): pl.pallas_call(image_kernel, out_shape=(jax.ShapeDtypeStruct((8, 4096), F...]
    all_to_all x1 -> x0, blocking collectives: 33.9 us -> none  [local(): lax.all_to_all(stacked.astype(jnp.bfloat16), ('vis', 'row'), split_axis=2...]
    dot_general x23 -> x2, matrix products: 23 us -> 2.61 us  [the longest x1 1.48 us: conv_weights(): jnp.einsum('bhr,rskj->kbshj', tap2, conv_two, preferred_element_type=F32)]
    all_to_all x2 -> x0, waiting for transfers between devices: 19.2 us -> none  [the longest x1 11.6 us: local(): lax.all_to_all(reduced.astype(jnp.bfloat16), 'col', split_axis=1, concat_...]
    ppermute x4 -> x0, starting transfers between devices: 17.7 us -> none  [the longest x2 13.9 us: with_halo(): lax.ppermute(head, axis, [((i + 1) % count, i) for i in range(ends)])]
    ppermute x4 -> x0, waiting for transfers between devices: 11.7 us -> none  [the longest x2 11.6 us: with_halo(): lax.ppermute(tail, axis, [(i, (i + 1) % count) for i in range(ends)])]
    all_to_all x2 -> x0, starting transfers between devices: 9.54 us -> none  [the longest x1 6.13 us: local(): lax.all_to_all(reduced.astype(jnp.bfloat16), 'col', split_axis=1, concat_...]
  transfers between devices with their start and end apart: 7 -> 0, of which waited for: 6 -> 0; matrix products, arithmetic and copies ran while one was open for 1% -> 0% of each run, Pallas kernels for 0% -> 0%
where the time goes in v1:
time: 89.5 us; the launch traced here: 89.2 us
  Pallas kernels  74.6 us (83%)
  local copies, waits for them, and re-layouts  10.7 us (12%)
  matrix products  2.61 us (3%)
  other arithmetic  1.15 us (1%)
    pallas_call x1, Pallas kernels, image_rows(): pl.pallas_call(image_kernel, out_shape=(jax.ShapeDtypeStruct((8, 4096), F...  67.5 us
    pallas_call x1, Pallas kernels, convolve(): pl.pallas_call(functools.partial(conv_kernel, chunk), out_shape=jax.Shape...  7.12 us
    reshape x1, local copies, waits for them, and re-layouts, conv_weights(): w2 = w2.astype(BF16).reshape(256, 960)  3.85 us
    unnamed x16, local copies, waits for them, and re-layouts  3.6 us
    convert_element_type x1, local copies, waits for them, and re-layouts, conv_weights(): w2 = w2.astype(BF16).reshape(256, 960)  2.52 us

profile of v1, /device:TPU:1, one launch (start us, length us, event | category | flops | bytes accessed | tf_op | source)
XLA Modules:
  0.0 89.2 jit_solution(9700125590976679514)
XLA Ops:
  0.0 0.1 and_convert_fusion
  0.1 0.1 and_convert_fusion.1
  0.2 0.9 broadcast_multiply_fusion
  1.1 1.1 %convert_bitcast_fusion.1 = (bf16[10,32,3,1,16]{1,4,2,0,3:T(8,128)(2,1)S(1)}, bf16[10,32,3,1,16]{1,4,2,0,3:T(8,128)(2,1)S(1)}) fusion(f32[10,16]{1,0:T(8,128)S(1)} %and_convert_fusion, f32[32,3,16]{0,2,1:T(8,128)S(1)} %broadcast_multiply_fusion, f32[32,3,3]{0,2,1:T(4,128)} %param.12, s32[10,3]{1,0:T(8,128)S(1)} %iota_add_fusion), kind=kOutput, calls=%fused_computation.9 | convolution fusion | flops 645600 | bytes 69496 | tf_op jit(solution)/shard_map/hir,krs->hksi/dot_general | solution.py:442
  2.2 0.0 copy-start.6
  2.2 0.1 pad_maximum_fusion
  2.3 0.1 copy.16
  2.5 0.3 reshape.133
  2.8 0.1 copy.19.w1
  2.9 0.0 copy-done.2
  2.9 0.0 copy-done
  2.9 0.0 copy-start.1
  3.0 1.2 %copy-done.1 = bf16[512,1024]{1,0:T(8,128)(2,1)S(1)} copy-done((bf16[512,1024]{1,0:T(8,128)(2,1)S(1)}, bf16[512,1024]{1,0:T(8,128)(2,1)}, u32[]{:S(2)}) %copy-start.1) | copy-done | bytes 1048600
  4.2 0.8 copy-done.3
  5.0 0.8 copy-done.4
  5.8 0.7 copy-done.5
  6.5 67.5 %image_rows.1 = (f32[8,4096]{1,0:T(8,128)S(1)}, f32[2,8,1024]{2,1,0:T(8,128)S(1)}) custom-call(bf16[2,512,1024]{2,1,0:T(8,128)(2,1)S(1)} %bitcast.38, s32[4,8]{1,0:T(4,128)S(1)} %bitcast.39, f32[16,1024]{1,0:T(8,128)S(1)} %copy-done.3, bf16[8,128,256]{2,1,0:T(8,128)(2,1)S(1)} %copy-done.2, bf16[512,1024]{1,0:T(8,128)(2,1)S(1)} %copy-done.1, ...), custom_call_target="tpu_custom_call" | custom-call | tf_op jit(solution)/shard_map/image_rows/pallas_call | solution.py:354
  74.0 0.0 copy-done.6
  74.0 1.5 %convert_bitcast_fusion = bf16[32,8,3,10,32]{4,3,0,2,1:T(8,128)(2,1)S(1)} fusion(bf16[3,3,32,32]{3,2,1,0:T(8,128)(2,1)S(1)} %copy-done.6, s32[8,3]{1,0:T(8,128)S(1)} %iota_add_fusion.1), kind=kOutput, calls=%fused_computation | convolution fusion | flops 1720560 | bytes 510048 | tf_op jit(solution)/shard_map/bhr,rskj->kbshj/dot_general | solution.py:453
  75.5 2.5 %copy.18 = bf16[32,8,3,10,32]{4,3,2,1,0:T(8,128)(2,1)} copy(bf16[32,8,3,10,32]{4,3,0,2,1:T(8,128)(2,1)S(1)} %convert_bitcast_fusion) | data formatting | bytes 983040 | tf_op jit(solution)/shard_map/convert_element_type | solution.py:454
  78.1 3.8 %reshape.134.w2 = bf16[256,960]{1,0:T(8,128)(2,1)S(1)} reshape(bf16[32,8,3,10,32]{4,3,2,1,0:T(8,128)(2,1)} %copy.18) | data formatting | bytes 983040 | tf_op jit(solution)/shard_map/reshape | solution.py:454
  81.9 0.1 broadcast_in_dim.2
  82.0 0.1 broadcast_in_dim_reshape.4.b2
  82.1 7.1 %convolve.1 = bf16[32,8,4096]{2,1,0:T(8,128)(2,1)} custom-call(f32[8,4096]{1,0:T(8,128)S(1)} %get-tuple-element.7.image, f32[2,8,1024]{2,1,0:T(8,128)S(1)} %get-tuple-element.8.halo, bf16[320,144]{1,0:T(8,128)(2,1)S(1)} %copy.19.w1, bf16[256,960]{1,0:T(8,128)(2,1)S(1)} %reshape.134.w2, f32[256,1]{1,0:T(8,128)S(1)} %broadcast_in_dim_reshape.4.b2), custom_call_target="tpu_custom_call" | custom-call | tf_op jit(solution)/shard_map/convolve/pallas_call | solution.py:463
  (13 shorter events, 0.1 us)
Async XLA Ops:
  0.0 2.9 %copy-start.2 = (bf16[8,128,256]{2,1,0:T(8,128)(2,1)S(1)}, bf16[8,128,256]{2,1,0:T(8,128)(2,1)}, u32[]{:S(2)}) copy-start(bf16[8,128,256]{2,1,0:T(8,128)(2,1)} %constant.55.clone.mat_h) | copy-start | bytes 1572868
  0.0 2.9 %copy-start = (bf16[1,2,512,1024]{3,2,1,0:T(8,128)(2,1)S(1)}, bf16[1,2,512,1024]{3,2,1,0:T(8,128)(2,1)}, u32[]{:S(2)}) copy-start(bf16[1,2,512,1024]{3,2,1,0:T(8,128)(2,1)} %param.10) | copy-start | bytes 6291460
  2.2 71.8 %copy-start.6 = (bf16[3,3,32,32]{3,2,1,0:T(8,128)(2,1)S(1)}, bf16[3,3,32,32]{3,2,1,0:T(8,128)(2,1)}, u32[]{:S(2)}) copy-start(bf16[3,3,32,32]{3,2,1,0:T(8,128)(2,1)} %param.14) | copy-start | bytes 55300
  2.9 1.2 %copy-start.1 = (bf16[512,1024]{1,0:T(8,128)(2,1)S(1)}, bf16[512,1024]{1,0:T(8,128)(2,1)}, u32[]{:S(2)}) copy-start(bf16[512,1024]{1,0:T(8,128)(2,1)} %constant.56.clone.cs_h) | copy-start | bytes 3145732
  4.2 0.8 copy-start.3
  5.0 0.8 copy-start.4
  5.8 0.7 copy-start.5
  78.1 3.9 %copy-start.7 = (f32[32]{0:T(128)S(1)}, f32[32]{0:T(128)}, u32[]{:S(2)}) copy-start(f32[32]{0:T(128)} %param.15) | copy-start | bytes 388

commit v2 on v1

v2 whole, which is shorter than its diff:
```python
import functools

import jax
import jax.numpy as jnp
import numpy as np
from jax import lax
from jax.experimental import pallas as pl
from jax.experimental.pallas import tpu as pltpu
from jax.sharding import PartitionSpec as P

MESH = pl.DeviceIdType.MESH
F32 = jnp.float32
BF16 = jnp.bfloat16
N = 8192
VMEM_LIMIT = 61 * 2**20
CHIP_ORDER = (
    (1, 0), (3, 0), (0, 1), (0, 3), (1, 1), (3, 3), (1, 3), (3, 1),
    (2, 0), (0, 2), (2, 1), (1, 2), (2, 3), (3, 2), (2, 2),
)
Z_ORDER = (8, 7, 9, 6, 10, 5, 11, 4, 12, 3, 13, 2, 14, 1, 15)


def tables():
    p = np.arange(1024)
    tw1 = np.zeros((16, 1024))
    for beta in range(8):
        ang = 2 * np.pi * p * beta / N
        tw1[2 * beta] = (-1) ** beta * np.cos(ang)
        tw1[2 * beta + 1] = (-1) ** beta * np.sin(ang)
    l = np.arange(128)
    mat = np.zeros((8, 64, 256))
    for bp in range(8):
        ang = 2 * np.pi * l * (8 * (np.arange(64)[:, None] - 32) + bp) / 1024
        mat[bp, :, :128] = np.cos(ang)
        mat[bp, :, 128:] = -np.sin(ang)
    k = np.arange(512)
    ang = 2 * np.pi * ((k[:, None] * k[None, :]) % 512) / 512
    cs = np.concatenate([np.cos(ang), np.sin(ang)], axis=1)
    tt = np.arange(16)
    ang = 2 * np.pi * tt[:, None] * k[None, :] / N
    sign = (1 - 2 * (k % 2)) / N
    tw2 = np.stack([np.cos(ang) * sign, np.sin(ang) * sign], axis=1).reshape(32, 512)
    return (
        jnp.asarray(tw1, F32),
        jnp.asarray(mat, BF16),
        jnp.asarray(cs, BF16),
        jnp.asarray(tw2, F32),
    )


def add(a, b):
    return (a[0] + b[0], a[1] + b[1])


def sub(a, b):
    return (a[0] - b[0], a[1] - b[1])


def add_i(a, b):
    return (a[0] - b[1], a[1] + b[0])


def sub_i(a, b):
    return (a[0] + b[1], a[1] - b[0])


def dft8(x):
    r = 0.5**0.5
    a0, a1, a2, a3 = add(x[0], x[4]), sub(x[0], x[4]), add(x[2], x[6]), sub(x[2], x[6])
    o0, o1, o2, o3 = add(x[1], x[5]), sub(x[1], x[5]), add(x[3], x[7]), sub(x[3], x[7])
    even = [add(a0, a2), add_i(a1, a3), sub(a0, a2), sub_i(a1, a3)]
    odd = [add(o0, o2), add_i(o1, o3), sub(o0, o2), sub_i(o1, o3)]
    w1 = ((odd[1][0] - odd[1][1]) * r, (odd[1][0] + odd[1][1]) * r)
    w3 = ((-odd[3][0] - odd[3][1]) * r, (odd[3][0] - odd[3][1]) * r)
    return [
        add(even[0], odd[0]), add(even[1], w1), add_i(even[2], odd[2]), add(even[3], w3),
        sub(even[0], odd[0]), sub(even[1], w1), sub_i(even[2], odd[2]), sub(even[3], w3),
    ]


def build_weights(linear, small, conv_two, w1, w2, base, wide):
    first = (linear == 0).astype(F32)
    final = (linear == 511).astype(F32)
    lane = lax.broadcasted_iota(jnp.int32, (32, 256), 1)
    taps = jnp.zeros((32, 256), F32)
    for r in range(3):
        for s in range(3):
            i = r * 3 + s
            taps = jnp.where(lane == s * 48 + r, small[:, i : i + 1], taps)

    def split(v):
        hi = v.astype(BF16).astype(F32)
        return hi, v - hi

    hi, lo = split(taps)
    taps = hi + pltpu.roll(hi, 16, 1) + pltpu.roll(lo, 32, 1)
    hi, lo = split(small[:, 9:10])
    shift = jnp.where(lane == 60, hi, 0.0) + jnp.where(lane == 92, lo, 0.0)
    place = lane % 16
    seen = 1.0 - first * (place < 2).astype(F32)
    seen = seen - final * ((place == 10) | (place == 11)).astype(F32)
    for hr in range(10):
        block = (pltpu.roll(taps, hr, 1) if hr else taps) + shift
        block = block * seen
        if hr == 0:
            block = block * (1.0 - first)
        if hr == 9:
            block = block * (1.0 - final)
        w1[hr * 32 : (hr + 1) * 32, :] = block[:, :144].astype(BF16)
    base[...] = jnp.zeros((32, 1024), F32)
    for r in range(3):
        for s in range(3):
            at = s * 320 + r * 32
            base[:, at : at + 32] = conv_two[r, s].astype(F32)
    hi, lo = split(small[:, 10:11])
    lane = lax.broadcasted_iota(jnp.int32, (32, 128), 1)
    offset = jnp.where(lane == 64, hi, 0.0) + jnp.where(lane == 65, lo, 0.0)
    for b in range(8):
        block = pltpu.roll(base[...], b * 32, 1) if b else base[...]
        for i in range(8):
            piece = block[:, i * 128 : (i + 1) * 128]
            if i == 7:
                piece = piece + offset
            wide[i, pl.ds(b, 32, stride=8), :] = piece
    for i in range(8):
        w2[:, i * 128 : (i + 1) * 128] = wide[i].astype(BF16)


def image_kernel(
    part, cover, tw1_h, mat_h, cs_h, tw2_h, small, conv_two,
    image, halo, w1, w2,
    xin, pair_out, pair_in, rows_out, rows_in, mid, spec, slab_out, slab_in, slab_f, z_out, z_in, acc,
    halo_out, tw1, mat, cs, tw2, base, wide,
    sem_in, sem_tab, ps, pr, cs_s, cr, ss, sr, zs, zr, hs, hr, near,
):
    vis = lax.axis_index("vis")
    row = lax.axis_index("row")
    col = lax.axis_index("col")
    core = vis % 2
    ylo = vis // 2
    x = col % 4
    y = (col // 4) * 2 + ylo
    chip = ylo * 8 + col
    mine = core * 16 + chip
    linear = vis * 128 + row * 8 + col

    def at(v, r, c):
        return {"vis": v, "row": r, "col": c}

    def chip_of(dx, dy):
        xx, yy = (x + dx) % 4, (y + dy) % 4
        return yy % 2, (yy // 2) * 4 + xx

    def neighbour(step):
        n = (linear + step) % 512
        return at(n // 128, (n // 8) % 16, n % 8)

    def along(dz):
        return at(vis, (row + dz) % 16, col)

    def send(src, dst, send_sem, recv_sem, peer):
        c = pltpu.make_async_remote_copy(
            src_ref=src, dst_ref=dst, send_sem=send_sem, recv_sem=recv_sem,
            device_id=peer, device_id_type=MESH,
        )
        c.start()
        return c

    def spread_word(level):
        for dz in (2**level, 16 - 2**level):
            pl.semaphore_signal(near.at[level], inc=1, device_id=along(dz), device_id_type=MESH)

    partner = at(vis + 1 - 2 * core, row, col)
    chips = [chip_of(dx, dy) for dx, dy in CHIP_ORDER]
    slab = [partner]
    for cy, cc in chips:
        slab.append(at(cy * 2 + core, row, cc))
        slab.append(at(cy * 2 + 1 - core, row, cc))
    after, before = neighbour(1), neighbour(511)

    barrier = pltpu.get_barrier_semaphore()
    greeted = [along(1), along(15), after, before] + slab
    for peer in greeted:
        pl.semaphore_signal(barrier, inc=1, device_id=peer, device_id_type=MESH)

    def rows_of(half, blk):
        return pl.ds(pl.multiple_of(half * 256 + blk * 128, 128), 128)

    loads = []
    for h, half in enumerate((1 - core, core)):
        for blk in range(2):
            for ri in range(2):
                slot = h * 4 + blk * 2 + ri
                c = pltpu.make_async_copy(
                    part.at[ri, rows_of(half, blk)], xin.at[slot], sem_in.at[slot]
                )
                c.start()
                loads.append(c)
    tabs = [
        pltpu.make_async_copy(src, dst, sem_tab.at[i])
        for i, (src, dst) in enumerate(((tw1_h, tw1), (mat_h, mat), (cs_h, cs), (tw2_h, tw2)))
    ]
    for c in tabs:
        c.start()

    def masked(slot, half, blk, dst, dslot):
        def one(j, carry):
            lanes = pl.ds(pl.multiple_of(j * 128, 128), 128)
            m = jnp.full((128, 128), cover[half * 2 + blk, j].astype(F32)).astype(BF16)
            dst[dslot, :, lanes] = xin[slot, :, lanes] * m
            return carry

        lax.fori_loop(0, 8, one, 0)

    for blk in range(2):
        for ri in range(2):
            slot = blk * 2 + ri
            loads[slot].wait()
            masked(slot, 1 - core, blk, pair_out, slot)
    pl.semaphore_wait(barrier, len(greeted))
    spread_word(0)
    sends = [
        send(pair_out.at[slot], pair_in.at[slot], ps.at[slot], pr.at[slot], partner)
        for slot in range(4)
    ]
    for blk in range(2):
        for ri in range(2):
            slot = blk * 2 + ri
            loads[4 + slot].wait()
            masked(4 + slot, core, blk, xin, 4 + slot)
    for blk in range(2):
        a, b = blk * 2, blk * 2 + 1
        sends[a].wait_recv()
        sends[b].wait_recv()

        def one(i, carry):
            r = pl.ds(pl.multiple_of(i * 16, 16), 16)
            re = xin[4 + a, r, :].astype(F32) + pair_in[a, r, :].astype(F32)
            im = xin[4 + b, r, :].astype(F32) + pair_in[b, r, :].astype(F32)
            rows_out[0, blk * 8 + i] = jnp.concatenate([re[:8], im[:8]], axis=0).astype(BF16)
            rows_out[1, blk * 8 + i] = jnp.concatenate([re[8:], im[8:]], axis=0).astype(BF16)
            return carry

        lax.fori_loop(0, 8, one, 0)

    chip_sends = []
    for h in range(2):
        batch = []
        for i, (cy, cc) in enumerate(chips):
            peer = at(cy * 2 + core, row, cc)
            src, dst = rows_out.at[h, cy * 8 + cc], rows_in.at[h, chip]
            batch.append(send(src, dst, cs_s.at[h * 15 + i], cr.at[h * 15 + i], peer))
        chip_sends.append(batch)
    for h in range(2):
        rows_in[h, chip] = rows_out[h, chip]
    pl.semaphore_wait(near.at[0], 2)
    spread_word(1)
    build_weights(linear, small, conv_two, w1, w2, base, wide)
    pl.semaphore_wait(near.at[1], 2)
    spread_word(2)
    for c in tabs:
        c.wait()

    places = []
    for cy, cc in chips:
        places.append((cy * 2 + core, cc))
        places.append((cy * 2 + 1 - core, cc))
    places.append((vis + 1 - 2 * core, col))

    def transform(h):
        def stage_one(q, carry):
            lanes = pl.ds(pl.multiple_of(q * 128, 128), 128)
            xs = []
            for c in range(8):
                v = rows_in[h, c, :, lanes].astype(F32) + rows_in[h, 8 + c, :, lanes].astype(F32)
                xs.append((v[:8], v[8:]))
            for beta, (re, im) in enumerate(dft8(xs)):
                wr = jnp.broadcast_to(tw1[2 * beta : 2 * beta + 1, lanes], (8, 128))
                wi = jnp.broadcast_to(tw1[2 * beta + 1 : 2 * beta + 2, lanes], (8, 128))
                mid[beta, q, 0] = re * wr - im * wi
                mid[beta, q, 1] = re * wi + im * wr
            return carry

        lax.fori_loop(0, 8, stage_one, 0)

        def stage_two(g, carry):
            low = dft8([(mid[2 * g, q, 0], mid[2 * g, q, 1]) for q in range(8)])
            high = dft8([(mid[2 * g + 1, q, 0], mid[2 * g + 1, q, 1]) for q in range(8)])
            top = pl.ds(pl.multiple_of(g * 16, 16), 16)
            bot = pl.ds(pl.multiple_of(64 + g * 16, 16), 16)
            for bp in range(8):
                re = jnp.concatenate([low[bp][0], high[bp][0]], axis=0)
                im = jnp.concatenate([low[bp][1], high[bp][1]], axis=0)
                spec[bp, top, 0:128] = re.astype(BF16)
                spec[bp, top, 128:256] = im.astype(BF16)
                spec[bp, bot, 0:128] = im.astype(BF16)
                spec[bp, bot, 128:256] = (-re).astype(BF16)
            return carry

        lax.fori_loop(0, 4, stage_two, 0)

        def stage_three(bp, carry):
            out = lax.dot_general(
                mat[bp], spec[bp], (((1,), (1,)), ((), ())), preferred_element_type=F32
            ).astype(BF16)
            for v in range(4):
                slab_out[h, v * 8 + bp] = out[v * 16 : (v + 1) * 16]
            return carry

        lax.fori_loop(0, 8, stage_three, 0)
        batch = []
        for i, (v, c_) in enumerate(places):
            src, dst = slab_out.at[h, v * 8 + c_], slab_in.at[h, mine]
            batch.append(send(src, dst, ss.at[h * 31 + i], sr.at[h * 31 + i], at(v, row, c_)))
        slab_in[h, mine] = slab_out[h, vis * 8 + col]
        return batch

    def forward(h):
        def widen(d, carry):
            slab_f[pl.ds(pl.multiple_of(d * 16, 16), 16), :] = slab_in[h, d].astype(F32)
            return carry

        lax.fori_loop(0, 32, widen, 0)
        for z in range(16):
            z_out[h, z] = slab_f[pl.ds(z, 32, stride=16), :].astype(BF16)
        batch = []
        for i, dz in enumerate(Z_ORDER):
            src, dst = z_out.at[h, (row + dz) % 16], z_in.at[h, row]
            batch.append(send(src, dst, zs.at[h * 15 + i], zr.at[h * 15 + i], along(dz)))
        z_in[h, row] = z_out[h, row]
        return batch

    def collect(h):
        out = lax.dot_general(
            z_in[h].reshape(512, 128), cs[...], (((0,), (0,)), ((), ())),
            preferred_element_type=F32,
        )
        for i in range(8):
            acc[h, i] = out[:, i * 128 : (i + 1) * 128]

    slab_sends, z_sends = [], []
    for h in range(2):
        for c in chip_sends[h]:
            c.wait_recv()
        slab_sends.append(transform(h))
        for c in slab_sends[h]:
            c.wait_recv()
        if h == 0:
            pl.semaphore_wait(near.at[2], 2)
        z_sends.append(forward(h))
    for h in range(2):
        for c in z_sends[h]:
            c.wait_recv()
        collect(h)

    def last(q, carry):
        lo = pl.ds(pl.multiple_of(q * 128, 128), 128)
        vs = []
        for tt in range(16):
            h, t = tt // 8, tt % 8
            top, bot = pl.ds(t, 8, stride=8), pl.ds(64 + t, 8, stride=8)
            re = acc[h, q, top, :] - acc[h, 4 + q, bot, :]
            im = acc[h, 4 + q, top, :] + acc[h, q, bot, :]
            wr = jnp.broadcast_to(tw2[2 * tt : 2 * tt + 1, lo], (8, 128))
            wi = jnp.broadcast_to(tw2[2 * tt + 1 : 2 * tt + 2, lo], (8, 128))
            vs.append((re * wr - im * wi, re * wi + im * wr))
        even = dft8([add(vs[t], vs[t + 8]) for t in range(8)])
        turned = []
        for t in range(8):
            a, b = float(np.cos(np.pi * t / 8)), float(np.sin(np.pi * t / 8))
            re, im = sub(vs[t], vs[t + 8])
            turned.append((re * a - im * b, re * b + im * a))
        odd = dft8(turned)
        for i, k in enumerate((6, 7, 0, 1)):
            image[:, pl.ds(pl.multiple_of((2 * i) * 512 + q * 128, 128), 128)] = even[k][0]
            image[:, pl.ds(pl.multiple_of((2 * i + 1) * 512 + q * 128, 128), 128)] = odd[k][0]
        return carry

    lax.fori_loop(0, 4, last, 0)

    for i in range(2):
        for j in range(4):
            lanes = slice(j * 1024, (j + 1) * 1024)
            halo_out[0, i * 4 + j : i * 4 + j + 1, :] = image[i : i + 1, lanes]
            halo_out[1, i * 4 + j : i * 4 + j + 1, :] = image[6 + i : 7 + i, lanes]
    halo_sends = [
        send(halo_out.at[i], halo.at[1 - i], hs.at[i], hr.at[i], peer)
        for i, peer in enumerate((before, after))
    ]
    for batch in [sends] + chip_sends + slab_sends + z_sends:
        for c in batch:
            c.wait_send()
    for c in halo_sends:
        c.wait()


def image_rows(partials, coverage, small, conv_two):
    any_spec = pl.BlockSpec(memory_space=pl.ANY)
    vmem = pl.BlockSpec(memory_space=pltpu.VMEM)
    dma = pltpu.SemaphoreType.DMA
    return pl.pallas_call(
        image_kernel,
        out_shape=(
            jax.ShapeDtypeStruct((8, 4096), F32),
            jax.ShapeDtypeStruct((2, 8, 1024), F32),
            jax.ShapeDtypeStruct((320, 144), BF16),
            jax.ShapeDtypeStruct((256, 1024), BF16),
        ),
        in_specs=[any_spec, pl.BlockSpec(memory_space=pltpu.SMEM)] + [any_spec] * 4 + [vmem] * 2,
        out_specs=(vmem,) * 4,
        scratch_shapes=[
            pltpu.VMEM((8, 128, 1024), BF16),
            pltpu.VMEM((4, 128, 1024), BF16),
            pltpu.VMEM((4, 128, 1024), BF16),
            pltpu.VMEM((2, 16, 16, 1024), BF16),
            pltpu.VMEM((2, 16, 16, 1024), BF16),
            pltpu.VMEM((8, 8, 2, 8, 128), F32),
            pltpu.VMEM((8, 128, 256), BF16),
            pltpu.VMEM((2, 32, 16, 128), BF16),
            pltpu.VMEM((2, 32, 16, 128), BF16),
            pltpu.VMEM((512, 128), F32),
            pltpu.VMEM((2, 16, 32, 128), BF16),
            pltpu.VMEM((2, 16, 32, 128), BF16),
            pltpu.VMEM((2, 8, 128, 128), F32),
            pltpu.VMEM((2, 8, 1024), F32),
            pltpu.VMEM((16, 1024), F32),
            pltpu.VMEM((8, 64, 256), BF16),
            pltpu.VMEM((512, 1024), BF16),
            pltpu.VMEM((32, 512), F32),
            pltpu.VMEM((32, 1024), F32),
            pltpu.VMEM((8, 256, 128), F32),
            dma((8,)), dma((4,)), dma((4,)), dma((4,)), dma((30,)), dma((30,)),
            dma((62,)), dma((62,)), dma((30,)), dma((30,)), dma((2,)), dma((2,)),
            pltpu.SemaphoreType.REGULAR((3,)),
        ],
        name="image_rows",
        compiler_params=pltpu.CompilerParams(
            collective_id=0, has_side_effects=True, vmem_limit_bytes=VMEM_LIMIT
        ),
    )(partials, coverage, *tables(), small, conv_two)


def conv_kernel(chunk, image, halo, w1, w2, out, ext, shifted):
    width = image.shape[1]
    step = pl.program_id(0)

    @pl.when(step == 0)
    def _():
        ext[2:10, :] = image[...]
        for i in range(2):
            for j in range(4):
                lanes = slice(j * 1024, (j + 1) * 1024)
                ext[i : i + 1, lanes] = halo[0, i * 4 + j : i * 4 + j + 1, :]
                ext[10 + i : 11 + i, lanes] = halo[1, i * 4 + j : i * 4 + j + 1, :]
        ext[12:16, :] = jnp.ones((4, width), F32)
        full = ext[...]
        lane = lax.broadcasted_iota(jnp.int32, full.shape, 1)
        for i, delta in enumerate(range(-2, 3)):
            v = full
            if delta:
                inside = (lane + delta >= 0) & (lane + delta < width)
                v = jnp.where(inside, pltpu.roll(full, (-delta) % width, 1), 0.0)
            hi = v.astype(BF16)
            lo = (v - hi.astype(F32)).astype(BF16)
            shifted[i * 48 : i * 48 + 16, :] = hi
            shifted[i * 48 + 16 : i * 48 + 32, :] = lo
            shifted[i * 48 + 32 : i * 48 + 48, :] = hi

    lanes = pl.ds(pl.multiple_of(step * chunk, chunk), chunk)
    place = step * chunk + lax.broadcasted_iota(jnp.int32, (320, 128), 1)
    parts = []
    for s in range(3):
        h = jnp.dot(w1[...], shifted[s * 48 : s * 48 + 144, lanes], preferred_element_type=F32)
        h = jnp.maximum(h, 0.0)
        if s == 0:
            edge = jnp.where(place > 0, h[:, :128], 0.0)
            h = jnp.concatenate([edge, h[:, 128:]], axis=1)
        if s == 2:
            edge = jnp.where(place + (chunk - 128) < width - 1, h[:, chunk - 128 :], 0.0)
            h = jnp.concatenate([h[:, : chunk - 128], edge], axis=1)
        parts.append(h.astype(BF16))
    parts.append(jnp.ones((64, chunk), BF16))
    hidden = jnp.concatenate(parts, axis=0)
    o = jnp.dot(w2[...], hidden, preferred_element_type=F32)
    out[...] = o.reshape(32, 8, chunk).astype(BF16)


def convolve(image, halo, w1, w2):
    chunk = 512
    vmem = pl.BlockSpec(memory_space=pltpu.VMEM)
    return pl.pallas_call(
        functools.partial(conv_kernel, chunk),
        grid=(4096 // chunk,),
        out_shape=jax.ShapeDtypeStruct((32, 8, 4096), BF16),
        in_specs=[vmem] * 4,
        out_specs=pl.BlockSpec((32, 8, chunk), lambda c: (0, 0, c)),
        scratch_shapes=[pltpu.VMEM((16, 4096), F32), pltpu.VMEM((240, 4096), BF16)],
        name="convolve",
        compiler_params=pltpu.CompilerParams(vmem_limit_bytes=40 * 2**20),
    )(image, halo, w1, w2)


def local(partials, coverage, conv_one, bias_one, conv_two, bias_two):
    small = jnp.concatenate(
        [conv_one.reshape(32, 9), bias_one[:, None], bias_two[:, None]], axis=1
    )
    image, halo, w1, w2 = image_rows(partials[0], coverage[0], small, conv_two)
    return convolve(image, halo, w1, w2)


def solution(mesh):
    placed = (P("vis", None, "row", "col"), P("vis", "row", "col"), P(), P(), P(), P())
    return jax.shard_map(
        local,
        mesh=mesh,
        in_specs=placed,
        out_specs=P(None, ("vis", "row", "col"), None),
        check_vma=False,
    )
```

time: 89.5 us -> 76.8 us (0.86)
  Pallas kernels: 74.6 us -> 69.8 us
  local copies, waits for them, and re-layouts: 10.7 us -> 5.95 us
  matrix products: 2.61 us -> 0 us
    pallas_call x1, Pallas kernels: 67.5 us -> 63.2 us  [image_rows(): pl.pallas_call(image_kernel, out_shape=(jax.ShapeDtypeStruct((8, 4096), F...]
    reshape x3 -> x2, local copies, waits for them, and re-layouts: 4.3 us -> 0.79 us  [local(): conv_one.reshape(32, 9)]
    dot_general x2 -> x0, matrix products: 2.61 us -> none  [the longest x1 1.48 us: conv_weights(): jnp.einsum('bhr,rskj->kbshj', tap2, conv_two, preferred_element_type=F32)]
    convert_element_type x1 -> x0, local copies, waits for them, and re-layouts: 2.52 us -> none  [conv_weights(): w2 = w2.astype(BF16).reshape(256, 960)]
    broadcast_in_dim x1 -> x2, local copies, waits for them, and re-layouts: 0.07 us -> 1.47 us  [the longest x1 0.74 us: local(): bias_one[:, None]]
    unnamed x16 -> x8, local copies, waits for them, and re-layouts: 3.6 us -> 3.69 us
where the time goes in v2:
time: 76.8 us; the launch traced here: 76.4 us
  Pallas kernels  69.8 us (91%)
  local copies, waits for them, and re-layouts  5.95 us (8%)
    pallas_call x1, Pallas kernels, image_rows(): pl.pallas_call(image_kernel, out_shape=(jax.ShapeDtypeStruct((8, 4096), F...  63.2 us
    pallas_call x1, Pallas kernels, convolve(): pl.pallas_call(functools.partial(conv_kernel, chunk), grid=(4096 // chunk...  6.6 us
    unnamed x8, local copies, waits for them, and re-layouts  3.69 us

profile of v2, /device:TPU:1, one launch (start us, length us, event | category | flops | bytes accessed | tf_op | source)
XLA Modules:
  0.0 76.4 jit_solution(900392228522539380)
XLA Ops:
  0.0 0.7 reshape.3
  0.7 0.1 copy.14
  0.8 0.7 copy.15
  1.5 0.7 copy.16
  2.3 0.7 pad_maximum_fusion.small
  2.9 63.2 %image_rows.1 = (f32[8,4096]{1,0:T(8,128)}, f32[2,8,1024]{2,1,0:T(8,128)}, bf16[320,144]{1,0:T(8,128)(2,1)}, bf16[256,1024]{1,0:T(8,128)(2,1)}) custom-call(bf16[2,512,1024]{2,1,0:T(8,128)(2,1)} %bitcast.6, s32[4,8]{1,0:T(4,128)} %bitcast.7, f32[16,1024]{1,0:T(8,128)} %constant.8.clone.tw1_h, bf16[8,64,256]{2,1,0:T(8,128)(2,1)} %constant.9.clone.mat_h, ...), custom_call_target="tpu_custom_call" | custom-call | tf_op jit(solution)/shard_map/image_rows/pallas_call | solution.py:401
  66.1 0.0 copy-start
  66.1 1.0 %copy-done = bf16[256,1024]{1,0:T(8,128)(2,1)S(1)} copy-done((bf16[256,1024]{1,0:T(8,128)(2,1)S(1)}, bf16[256,1024]{1,0:T(8,128)(2,1)}, u32[]{:S(2)}) %copy-start) | copy-done | bytes 524312
  67.2 0.0 copy-start.1
  67.2 0.9 %copy-done.1 = bf16[320,144]{1,0:T(8,128)(2,1)S(1)} copy-done((bf16[320,144]{1,0:T(8,128)(2,1)S(1)}, bf16[320,144]{1,0:T(8,128)(2,1)}, u32[]{:S(2)}) %copy-start.1) | copy-done | bytes 92184
  68.1 0.0 copy-start.2
  68.1 0.9 %copy-done.2 = f32[8,4096]{1,0:T(8,128)S(1)} copy-done((f32[8,4096]{1,0:T(8,128)S(1)}, f32[8,4096]{1,0:T(8,128)}, u32[]{:S(2)}) %copy-start.2) | copy-done | bytes 131096
  69.0 0.0 copy-start.3
  69.0 0.8 %copy-done.3 = f32[2,8,1024]{2,1,0:T(8,128)S(1)} copy-done((f32[2,8,1024]{2,1,0:T(8,128)S(1)}, f32[2,8,1024]{2,1,0:T(8,128)}, u32[]{:S(2)}) %copy-start.3) | copy-done | bytes 65560
  69.8 6.6 %convolve.1 = bf16[32,8,4096]{2,1,0:T(8,128)(2,1)} custom-call(f32[8,4096]{1,0:T(8,128)S(1)} %copy-done.2, f32[2,8,1024]{2,1,0:T(8,128)S(1)} %copy-done.3, bf16[320,144]{1,0:T(8,128)(2,1)S(1)} %copy-done.1, bf16[256,1024]{1,0:T(8,128)(2,1)S(1)} %copy-done), custom_call_target="tpu_custom_call" | custom-call | tf_op jit(solution)/shard_map/convolve/pallas_call | solution.py:491
Async XLA Ops:
  66.1 1.0 %copy-start = (bf16[256,1024]{1,0:T(8,128)(2,1)S(1)}, bf16[256,1024]{1,0:T(8,128)(2,1)}, u32[]{:S(2)}) copy-start(bf16[256,1024]{1,0:T(8,128)(2,1)} %get-tuple-element.12.w2) | copy-start | bytes 1572868
  67.2 0.9 %copy-start.1 = (bf16[320,144]{1,0:T(8,128)(2,1)S(1)}, bf16[320,144]{1,0:T(8,128)(2,1)}, u32[]{:S(2)}) copy-start(bf16[320,144]{1,0:T(8,128)(2,1)} %get-tuple-element.11.w1) | copy-start | bytes 276484
  68.1 0.9 %copy-start.2 = (f32[8,4096]{1,0:T(8,128)S(1)}, f32[8,4096]{1,0:T(8,128)}, u32[]{:S(2)}) copy-start(f32[8,4096]{1,0:T(8,128)} %get-tuple-element.9.image) | copy-start | bytes 393220
  69.0 0.8 %copy-start.3 = (f32[2,8,1024]{2,1,0:T(8,128)S(1)}, f32[2,8,1024]{2,1,0:T(8,128)}, u32[]{:S(2)}) copy-start(f32[2,8,1024]{2,1,0:T(8,128)} %get-tuple-element.10.halo) | copy-start | bytes 196612

commit v3 on v2

--- a/solution.py
+++ b/solution.py
@@ -1,5 +1,3 @@
-import functools
-
 import jax
 import jax.numpy as jnp
 import numpy as np
@@ -78,60 +76,73 @@
     ]
 
 
-def build_weights(linear, small, conv_two, w1, w2, base, wide):
+def slot_of(hr, s):
+    if 2 <= hr < 8:
+        return s * 192 + (hr - 2) * 32
+    return 576 + s * 128 + (hr if hr < 2 else hr - 6) * 32
+
+
+def build_weights(linear, one_s, bias1_s, bias2_s, conv_two, w1, w2, taps, base, wide):
     first = (linear == 0).astype(F32)
     final = (linear == 511).astype(F32)
+    line = lax.broadcasted_iota(jnp.int32, (1, 256), 1)
+
+    def fill(k, carry):
+        v = jnp.zeros((1, 256), F32)
+        for r in range(3):
+            for s in range(3):
+                v = jnp.where(line == s * 48 + r, one_s[r, s, k], v)
+        v = jnp.where(line == 253, bias1_s[k], v)
+        taps[pl.ds(k, 1), :] = jnp.where(line == 254, bias2_s[k], v)
+        return carry
+
+    lax.fori_loop(0, 32, fill, 0)
     lane = lax.broadcasted_iota(jnp.int32, (32, 256), 1)
-    taps = jnp.zeros((32, 256), F32)
-    for r in range(3):
-        for s in range(3):
-            i = r * 3 + s
-            taps = jnp.where(lane == s * 48 + r, small[:, i : i + 1], taps)
 
     def split(v):
         hi = v.astype(BF16).astype(F32)
         return hi, v - hi
 
-    hi, lo = split(taps)
-    taps = hi + pltpu.roll(hi, 16, 1) + pltpu.roll(lo, 32, 1)
-    hi, lo = split(small[:, 9:10])
+    hi, lo = split(jnp.where(lane < 144, taps[...], 0.0))
+    spread = hi + pltpu.roll(hi, 16, 1) + pltpu.roll(lo, 32, 1)
+    hi, lo = split(taps[:, 253:254])
     shift = jnp.where(lane == 60, hi, 0.0) + jnp.where(lane == 92, lo, 0.0)
     place = lane % 16
     seen = 1.0 - first * (place < 2).astype(F32)
     seen = seen - final * ((place == 10) | (place == 11)).astype(F32)
     for hr in range(10):
-        block = (pltpu.roll(taps, hr, 1) if hr else taps) + shift
+        block = (pltpu.roll(spread, hr, 1) if hr else spread) + shift
         block = block * seen
         if hr == 0:
             block = block * (1.0 - first)
         if hr == 9:
             block = block * (1.0 - final)
-        w1[hr * 32 : (hr + 1) * 32, :] = block[:, :144].astype(BF16)
-    base[...] = jnp.zeros((32, 1024), F32)
-    for r in range(3):
         for s in range(3):
-            at = s * 320 + r * 32
-            base[:, at : at + 32] = conv_two[r, s].astype(F32)
-    hi, lo = split(small[:, 10:11])
+            at = slot_of(hr, s)
+            w1[at : at + 32, :] = (pltpu.roll(block, 48 * s, 1) if s else block).astype(BF16)
+    hi, lo = split(taps[:, 254:255])
     lane = lax.broadcasted_iota(jnp.int32, (32, 128), 1)
     offset = jnp.where(lane == 64, hi, 0.0) + jnp.where(lane == 65, lo, 0.0)
     for b in range(8):
-        block = pltpu.roll(base[...], b * 32, 1) if b else base[...]
+        base[...] = jnp.zeros((32, 1024), F32)
+        base[:, 896:1024] = offset
+        for r in range(3):
+            for s in range(3):
+                at = slot_of(b + r, s)
+                base[:, at : at + 32] = conv_two[r, s].astype(F32)
         for i in range(8):
-            piece = block[:, i * 128 : (i + 1) * 128]
-            if i == 7:
-                piece = piece + offset
-            wide[i, pl.ds(b, 32, stride=8), :] = piece
+            wide[i, pl.ds(b, 32, stride=8), :] = base[:, i * 128 : (i + 1) * 128]
     for i in range(8):
         w2[:, i * 128 : (i + 1) * 128] = wide[i].astype(BF16)
 
 
 def image_kernel(
-    part, cover, tw1_h, mat_h, cs_h, tw2_h, small, conv_two,
-    image, halo, w1, w2,
+    part, cover_h, tw1_h, mat_h, cs_h, tw2_h, one_h, bias1_h, two_h, bias2_h,
+    feats,
+    image, halo, w1, w2, cover, one_s, bias1_s, bias2_s, conv_two, taps, ext, shifted, hidden, partial, ready,
     xin, pair_out, pair_in, rows_out, rows_in, mid, spec, slab_out, slab_in, slab_f, z_out, z_in, acc,
     halo_out, tw1, mat, cs, tw2, base, wide,
-    sem_in, sem_tab, ps, pr, cs_s, cr, ss, sr, zs, zr, hs, hr, near,
+    sem_in, sem_tab, ps, pr, cs_s, cr, ss, sr, zs, zr, hs, hr, so, near,
 ):
     vis = lax.axis_index("vis")
     row = lax.axis_index("row")
@@ -198,10 +209,16 @@
                 loads.append(c)
     tabs = [
         pltpu.make_async_copy(src, dst, sem_tab.at[i])
-        for i, (src, dst) in enumerate(((tw1_h, tw1), (mat_h, mat), (cs_h, cs), (tw2_h, tw2)))
+        for i, (src, dst) in enumerate(
+            (
+                (cover_h, cover), (tw1_h, tw1), (mat_h, mat), (cs_h, cs), (tw2_h, tw2),
+                (one_h, one_s), (bias1_h, bias1_s), (two_h, conv_two), (bias2_h, bias2_s),
+            )
+        )
     ]
     for c in tabs:
         c.start()
+    tabs[0].wait()
 
     def masked(slot, half, blk, dst, dslot):
         def one(j, carry):
@@ -255,11 +272,16 @@
         rows_in[h, chip] = rows_out[h, chip]
     pl.semaphore_wait(near.at[0], 2)
     spread_word(1)
-    build_weights(linear, small, conv_two, w1, w2, base, wide)
+    for c in tabs[1:]:
+        c.wait()
+    build_weights(linear, one_s, bias1_s, bias2_s, conv_two, w1, w2, taps, base, wide)
+    shifted[240:256, :] = jnp.zeros((16, 4096), BF16)
+    hidden[960:1024, :] = jnp.ones((64, 4096), BF16)
+    ext[0:2, :] = jnp.zeros((2, 4096), F32)
+    ext[10:12, :] = jnp.zeros((2, 4096), F32)
+    ext[12:16, :] = jnp.ones((4, 4096), F32)
     pl.semaphore_wait(near.at[1], 2)
     spread_word(2)
-    for c in tabs:
-        c.wait()
 
     places = []
     for cy, cc in chips:
@@ -387,28 +409,100 @@
         send(halo_out.at[i], halo.at[1 - i], hs.at[i], hr.at[i], peer)
         for i, peer in enumerate((before, after))
     ]
+    chunk = 512
+    width = 4096
+
+    def shift_all():
+        full = ext[...]
+        lane = lax.broadcasted_iota(jnp.int32, full.shape, 1)
+        for i, delta in enumerate(range(-2, 3)):
+            v = full
+            if delta:
+                inside = (lane + delta >= 0) & (lane + delta < width)
+                v = jnp.where(inside, pltpu.roll(full, (-delta) % width, 1), 0.0)
+            hi = v.astype(BF16)
+            lo = (v - hi.astype(F32)).astype(BF16)
+            shifted[i * 48 : i * 48 + 16, :] = hi
+            shifted[i * 48 + 16 : i * 48 + 32, :] = lo
+            shifted[i * 48 + 32 : i * 48 + 48, :] = hi
+
+    def layer_one(c, start, per):
+        lanes = pl.ds(pl.multiple_of(c * chunk, chunk), chunk)
+        place = c * chunk + lax.broadcasted_iota(jnp.int32, (per, 128), 1)
+        h = jnp.dot(w1[start : start + 3 * per, :], shifted[:, lanes], preferred_element_type=F32)
+        h = jnp.maximum(h, 0.0)
+        for s in range(3):
+            v = h[s * per : (s + 1) * per]
+            if s == 0:
+                v = jnp.concatenate([jnp.where(place > 0, v[:, :128], 0.0), v[:, 128:]], axis=1)
+            if s == 2:
+                far = place + (chunk - 128) < width - 1
+                edge = jnp.where(far, v[:, chunk - 128 :], 0.0)
+                v = jnp.concatenate([v[:, : chunk - 128], edge], axis=1)
+            hidden[start + s * per : start + (s + 1) * per, lanes] = v.astype(BF16)
+        return lanes
+
+    ext[2:10, :] = image[...]
+    shift_all()
+
+    def inner(c, carry):
+        lanes = layer_one(c, 0, 192)
+        partial[c] = jnp.dot(w2[:, :576], hidden[:576, lanes], preferred_element_type=F32)
+        return carry
+
+    lax.fori_loop(0, width // chunk, inner, 0)
     for batch in [sends] + chip_sends + slab_sends + z_sends:
         for c in batch:
             c.wait_send()
     for c in halo_sends:
         c.wait()
-
-
-def image_rows(partials, coverage, small, conv_two):
+    for i in range(2):
+        for j in range(4):
+            lanes = slice(j * 1024, (j + 1) * 1024)
+            ext[i : i + 1, lanes] = halo[0, i * 4 + j : i * 4 + j + 1, :]
+            ext[10 + i : 11 + i, lanes] = halo[1, i * 4 + j : i * 4 + j + 1, :]
+    shift_all()
+
+    def write(c):
+        lanes = pl.ds(pl.multiple_of(c * chunk, chunk), chunk)
+        return pltpu.make_async_copy(ready.at[c], feats.at[:, :, lanes], so.at[c])
+
+    def outer(c, carry):
+        lanes = layer_one(c, 576, 128)
+        o = jnp.dot(w2[:, 576:], hidden[576:, lanes], preferred_element_type=F32) + partial[c]
+        ready[c] = o.reshape(32, 8, chunk).astype(BF16)
+        write(c).start()
+        return carry
+
+    lax.fori_loop(0, width // chunk, outer, 0)
+    for c in range(width // chunk):
+        write(c).wait()
+
+
+def image_features(partials, coverage, conv_one, bias_one, conv_two, bias_two):
     any_spec = pl.BlockSpec(memory_space=pl.ANY)
-    vmem = pl.BlockSpec(memory_space=pltpu.VMEM)
     dma = pltpu.SemaphoreType.DMA
     return pl.pallas_call(
         image_kernel,
-        out_shape=(
-            jax.ShapeDtypeStruct((8, 4096), F32),
-            jax.ShapeDtypeStruct((2, 8, 1024), F32),
-            jax.ShapeDtypeStruct((320, 144), BF16),
-            jax.ShapeDtypeStruct((256, 1024), BF16),
-        ),
-        in_specs=[any_spec, pl.BlockSpec(memory_space=pltpu.SMEM)] + [any_spec] * 4 + [vmem] * 2,
-        out_specs=(vmem,) * 4,
+        out_shape=jax.ShapeDtypeStruct((32, 8, 4096), BF16),
+        in_specs=[any_spec] * 10,
+        out_specs=any_spec,
         scratch_shapes=[
+            pltpu.VMEM((8, 4096), F32),
+            pltpu.VMEM((2, 8, 1024), F32),
+            pltpu.VMEM((960, 256), BF16),
+            pltpu.VMEM((256, 1024), BF16),
+            pltpu.SMEM((4, 8), jnp.int32),
+            pltpu.SMEM((3, 3, 32), F32),
+            pltpu.SMEM((32,), F32),
+            pltpu.SMEM((32,), F32),
+            pltpu.VMEM((3, 3, 32, 32), BF16),
+            pltpu.VMEM((32, 256), F32),
+            pltpu.VMEM((16, 4096), F32),
+            pltpu.VMEM((256, 4096), BF16),
+            pltpu.VMEM((1024, 4096), BF16),
+            pltpu.VMEM((8, 256, 512), F32),
+            pltpu.VMEM((8, 32, 8, 512), BF16),
             pltpu.VMEM((8, 128, 1024), BF16),
             pltpu.VMEM((4, 128, 1024), BF16),
             pltpu.VMEM((4, 128, 1024), BF16),
@@ -429,83 +523,20 @@
             pltpu.VMEM((32, 512), F32),
             pltpu.VMEM((32, 1024), F32),
             pltpu.VMEM((8, 256, 128), F32),
-            dma((8,)), dma((4,)), dma((4,)), dma((4,)), dma((30,)), dma((30,)),
-            dma((62,)), dma((62,)), dma((30,)), dma((30,)), dma((2,)), dma((2,)),
+            dma((8,)), dma((9,)), dma((4,)), dma((4,)), dma((30,)), dma((30,)),
+            dma((62,)), dma((62,)), dma((30,)), dma((30,)), dma((2,)), dma((2,)), dma((8,)),
             pltpu.SemaphoreType.REGULAR((3,)),
         ],
-        name="image_rows",
+        name="image_features",
         compiler_params=pltpu.CompilerParams(
             collective_id=0, has_side_effects=True, vmem_limit_bytes=VMEM_LIMIT
         ),
-    )(partials, coverage, *tables(), small, conv_two)
-
-
-def conv_kernel(chunk, image, halo, w1, w2, out, ext, shifted):
-    width = image.shape[1]
-    step = pl.program_id(0)
-
-    @pl.when(step == 0)
-    def _():
-        ext[2:10, :] = image[...]
-        for i in range(2):
-            for j in range(4):
-                lanes = slice(j * 1024, (j + 1) * 1024)
-                ext[i : i + 1, lanes] = halo[0, i * 4 + j : i * 4 + j + 1, :]
-                ext[10 + i : 11 + i, lanes] = halo[1, i * 4 + j : i * 4 + j + 1, :]
-        ext[12:16, :] = jnp.ones((4, width), F32)
-        full = ext[...]
-        lane = lax.broadcasted_iota(jnp.int32, full.shape, 1)
-        for i, delta in enumerate(range(-2, 3)):
-            v = full
-            if delta:
-                inside = (lane + delta >= 0) & (lane + delta < width)
-                v = jnp.where(inside, pltpu.roll(full, (-delta) % width, 1), 0.0)
-            hi = v.astype(BF16)
-            lo = (v - hi.astype(F32)).astype(BF16)
-            shifted[i * 48 : i * 48 + 16, :] = hi
-            shifted[i * 48 + 16 : i * 48 + 32, :] = lo
-            shifted[i * 48 + 32 : i * 48 + 48, :] = hi
-
-    lanes = pl.ds(pl.multiple_of(step * chunk, chunk), chunk)
-    place = step * chunk + lax.broadcasted_iota(jnp.int32, (320, 128), 1)
-    parts = []
-    for s in range(3):
-        h = jnp.dot(w1[...], shifted[s * 48 : s * 48 + 144, lanes], preferred_element_type=F32)
-        h = jnp.maximum(h, 0.0)
-        if s == 0:
-            edge = jnp.where(place > 0, h[:, :128], 0.0)
-            h = jnp.concatenate([edge, h[:, 128:]], axis=1)
-        if s == 2:
-            edge = jnp.where(place + (chunk - 128) < width - 1, h[:, chunk - 128 :], 0.0)
-            h = jnp.concatenate([h[:, : chunk - 128], edge], axis=1)
-        parts.append(h.astype(BF16))
-    parts.append(jnp.ones((64, chunk), BF16))
-    hidden = jnp.concatenate(parts, axis=0)
-    o = jnp.dot(w2[...], hidden, preferred_element_type=F32)
-    out[...] = o.reshape(32, 8, chunk).astype(BF16)
-
-
-def convolve(image, halo, w1, w2):
-    chunk = 512
-    vmem = pl.BlockSpec(memory_space=pltpu.VMEM)
-    return pl.pallas_call(
-        functools.partial(conv_kernel, chunk),
-        grid=(4096 // chunk,),
-        out_shape=jax.ShapeDtypeStruct((32, 8, 4096), BF16),
-        in_specs=[vmem] * 4,
-        out_specs=pl.BlockSpec((32, 8, chunk), lambda c: (0, 0, c)),
-        scratch_shapes=[pltpu.VMEM((16, 4096), F32), pltpu.VMEM((240, 4096), BF16)],
-        name="convolve",
-        compiler_params=pltpu.CompilerParams(vmem_limit_bytes=40 * 2**20),
-    )(image, halo, w1, w2)
+    )(partials, coverage, *tables(), conv_one, bias_one, conv_two, bias_two)
 
 
 def local(partials, coverage, conv_one, bias_one, conv_two, bias_two):
-    small = jnp.concatenate(
-        [conv_one.reshape(32, 9), bias_one[:, None], bias_two[:, None]], axis=1
-    )
-    image, halo, w1, w2 = image_rows(partials[0], coverage[0], small, conv_two)
-    return convolve(image, halo, w1, w2)
+    taps = conv_one.transpose(1, 2, 0)
+    return image_features(partials[0], coverage[0], taps, bias_one, conv_two, bias_two)
 
 
 def solution(mesh):

time: 76.8 us -> 70 us (0.911)
  Pallas kernels: 69.8 us -> 66.7 us
  local copies, waits for them, and re-layouts: 5.95 us -> 3.13 us
    pallas_call x2 -> x1, Pallas kernels: 69.8 us -> 66.7 us  [image_features(): pl.pallas_call(image_kernel, out_shape=jax.ShapeDtypeStruct((32, 8, 4096)...]
    broadcast_in_dim x2 -> x0, local copies, waits for them, and re-layouts: 1.47 us -> none  [the longest x1 0.74 us: local(): bias_one[:, None]]
    reshape x2 -> x0, local copies, waits for them, and re-layouts: 0.79 us -> none  [local(): conv_one.reshape(32, 9)]
    unnamed x8 -> x1, local copies, waits for them, and re-layouts: 3.69 us -> 3.13 us
where the time goes in v3:
time: 70 us; the launch traced here: 69.9 us
  Pallas kernels  66.7 us (95%)
  local copies, waits for them, and re-layouts  3.13 us (4%)
    pallas_call x1, Pallas kernels, image_features(): pl.pallas_call(image_kernel, out_shape=jax.ShapeDtypeStruct((32, 8, 4096)...  66.7 us
    unnamed x1, local copies, waits for them, and re-layouts  3.13 us

profile of v3, /device:TPU:1, one launch (start us, length us, event | category | flops | bytes accessed | tf_op | source)
XLA Modules:
  0.0 69.9 jit_solution(6354046032409234349)
XLA Ops:
  0.0 66.7 %image_features.1 = bf16[32,8,4096]{2,1,0:T(8,128)(2,1)} custom-call(bf16[2,512,1024]{2,1,0:T(8,128)(2,1)} %bitcast.3, s32[4,8]{1,0:T(4,128)} %bitcast.5, f32[16,1024]{1,0:T(8,128)} %constant.8.clone.tw1_h, bf16[8,64,256]{2,1,0:T(8,128)(2,1)} %constant.9.clone.mat_h, bf16[512,1024]{1,0:T(8,128)(2,1)} %constant.10.clone.cs_h, ...), custom_call_target="tpu_custom_call" | custom-call | tf_op jit(solution)/shard_map/image_features/pallas_call | solution.py:485
  66.7 3.1 %copy.12 = bf16[32,8,4096]{2,1,0:T(8,128)(2,1)} copy(bf16[32,8,4096]{2,1,0:T(8,128)(2,1)} %image_features.1) | data formatting | bytes 4194304

commit v4 on v3

--- a/solution.py
+++ b/solution.py
@@ -365,10 +365,10 @@
         for c in chip_sends[h]:
             c.wait_recv()
         slab_sends.append(transform(h))
+    pl.semaphore_wait(near.at[2], 2)
+    for h in range(2):
         for c in slab_sends[h]:
             c.wait_recv()
-        if h == 0:
-            pl.semaphore_wait(near.at[2], 2)
         z_sends.append(forward(h))
     for h in range(2):
         for c in z_sends[h]:
@@ -534,9 +534,36 @@
     )(partials, coverage, *tables(), conv_one, bias_one, conv_two, bias_two)
 
 
+def hand_over_kernel(src, dst, buf, ins, outs):
+    loads = [pltpu.make_async_copy(src.at[pl.ds(i * 4, 4)], buf.at[i], ins.at[i]) for i in range(8)]
+    stores = [pltpu.make_async_copy(buf.at[i], dst.at[pl.ds(i * 4, 4)], outs.at[i]) for i in range(8)]
+    for c in loads:
+        c.start()
+    for i in range(8):
+        loads[i].wait()
+        stores[i].start()
+    for c in stores:
+        c.wait()
+
+
+def hand_over(features):
+    any_spec = pl.BlockSpec(memory_space=pl.ANY)
+    dma = pltpu.SemaphoreType.DMA
+    return pl.pallas_call(
+        hand_over_kernel,
+        out_shape=jax.ShapeDtypeStruct(features.shape, features.dtype),
+        in_specs=[any_spec],
+        out_specs=any_spec,
+        scratch_shapes=[pltpu.VMEM((8, 4, 8, 4096), BF16), dma((8,)), dma((8,))],
+        name="hand_over",
+        compiler_params=pltpu.CompilerParams(vmem_limit_bytes=VMEM_LIMIT),
+    )(features)
+
+
 def local(partials, coverage, conv_one, bias_one, conv_two, bias_two):
     taps = conv_one.transpose(1, 2, 0)
-    return image_features(partials[0], coverage[0], taps, bias_one, conv_two, bias_two)
+    out = image_features(partials[0], coverage[0], taps, bias_one, conv_two, bias_two)
+    return hand_over(out)
 
 
 def solution(mesh):

time: 70 us -> 67.1 us (0.959)
  local copies, waits for them, and re-layouts: 3.13 us -> 0 us
    unnamed x1 -> x0, local copies, waits for them, and re-layouts: 3.13 us -> none
    pallas_call x0 -> x1, Pallas kernels: none -> 2.39 us  [hand_over(): pl.pallas_call(hand_over_kernel, out_shape=jax.ShapeDtypeStruct(features....]
    pallas_call x1, Pallas kernels: 66.7 us -> 64.6 us  [image_features(): pl.pallas_call(image_kernel, out_shape=jax.ShapeDtypeStruct((32, 8, 4096)...]
where the time goes in v4:
time: 67.1 us; the launch traced here: 67 us
  Pallas kernels  67 us (100%)
    pallas_call x1, Pallas kernels, image_features(): pl.pallas_call(image_kernel, out_shape=jax.ShapeDtypeStruct((32, 8, 4096)...  64.6 us
    pallas_call x1, Pallas kernels, hand_over(): pl.pallas_call(hand_over_kernel, out_shape=jax.ShapeDtypeStruct(features....  2.39 us

profile of v4, /device:TPU:1, one launch (start us, length us, event | category | flops | bytes accessed | tf_op | source)
XLA Modules:
  0.0 67.0 jit_solution(1625714738100292559)
XLA Ops:
  0.0 64.6 %image_features.1.src = bf16[32,8,4096]{2,1,0:T(8,128)(2,1)} custom-call(bf16[2,512,1024]{2,1,0:T(8,128)(2,1)} %bitcast.3, s32[4,8]{1,0:T(4,128)} %bitcast.5, f32[16,1024]{1,0:T(8,128)} %constant.8.clone.tw1_h, bf16[8,64,256]{2,1,0:T(8,128)(2,1)} %constant.9.clone.mat_h, bf16[512,1024]{1,0:T(8,128)(2,1)} %constant.10.clone.cs_h, ...), custom_call_target="tpu_custom_call" | custom-call | tf_op jit(solution)/shard_map/image_features/pallas_call | solution.py:485
  64.6 2.4 %hand_over.1 = bf16[32,8,4096]{2,1,0:T(8,128)(2,1)} custom-call(bf16[32,8,4096]{2,1,0:T(8,128)(2,1)} %image_features.1.src), custom_call_target="tpu_custom_call" | custom-call | tf_op jit(solution)/shard_map/hand_over/pallas_call | solution.py:552
